TPU v7x, 32 devices: a whole 2x2x4 slice. The times are simulated.
32 devices in a mesh: rows: 8 (over y, x, core), feat: 4 (over z).
Axes of the slice: x: 2, y: 2, z: 4, core: 2. Of those that a mesh axis runs over, the one named last changes fastest.
Arguments:
- features: bfloat16 [1536, 16384], P('rows', 'feat'), may hold values from -0.5 to 0.5
- labels: int32 [1536], P('rows'), may hold values 0 or 1
- posterior: bfloat16 [16384], P('feat'), may hold values from -1 to 1
- prior_prec: float32 [16384], P('feat'), may hold values from 1 to 10
Outputs:
- hessian: float32 [16384, 16384], P('feat', 'rows')
- gradient: float32 [16384], P('feat')
All inputs are finite; a program needn't handle non-finite values. No bound on the sum of `labels` on one device may be relied on, other than what follows from the above.
Results may differ from a plain program's by a relative error of at most 0.003.
Values may be sent and summed in bfloat16 or wider, within the bound.
A program may use at most 128 MiB of HBM per device.

v0:
```python
import functools

import jax
import jax.numpy as jnp
from jax import lax
from jax.experimental import pallas as pl
from jax.experimental.pallas import tpu as pltpu
from jax.sharding import PartitionSpec as P

MESH = pl.DeviceIdType.MESH
SPLIT = 2


def gather_kernel(
    row_count, feat_count, x_ref, st_ref, all_ref, col_ref, stat_ref,
    ring, zs, zr, ps, pr, ds, dr, cs, cr, cl, ss, sr, ts, tr, lsem,
):
    r = lax.axis_index("rows")
    f = lax.axis_index("feat")
    n, width = x_ref.shape
    half = width // 2
    col_width = col_ref.shape[1]
    unit = min(col_width, half)
    per_half = half // unit
    per_owner = col_width // unit
    chips = row_count // 2
    bits = chips.bit_length() - 1
    part = n // SPLIT

    def rows_of(device):
        return pl.ds(pl.multiple_of(device * n, n), n)

    def remote(src, dst, send, recv, **where):
        return pltpu.make_async_remote_copy(
            src_ref=src, dst_ref=dst, send_sem=send, recv_sem=recv,
            device_id=where, device_id_type=MESH,
        )

    sends = []

    def go(copy):
        copy.start()
        sends.append(copy)

    def ring_slice(step, h, k):
        rows, cols = pl.ds(k * part, part), pl.ds(h * half, half)
        return x_ref.at[rows, cols] if step == 0 else ring.at[step - 1, rows, cols]

    def ring_copy(step, h, k):
        to = lax.rem(f + (1 if h == 0 else feat_count - 1), feat_count)
        return remote(
            ring_slice(step, h, k),
            ring.at[step, pl.ds(k * part, part), pl.ds(h * half, half)],
            zs.at[step, h, k], zr.at[step, h, k], feat=to,
        )

    def column_sends(step, h, k, start):
        block = lax.rem(f + (feat_count - step if h == 0 else step), feat_count)
        for u in range(per_half):
            inner = h * half + u * unit
            if width % col_width == 0:
                owner = block * (width // col_width) + inner // col_width
                offset = inner % col_width
                slot = offset // unit
            else:
                owner = (block * width + inner) // col_width
                slot = ((block * width + inner) % col_width) // unit
                offset = pl.multiple_of(slot * unit, unit)
            src = ring_slice(step, h, k).at[:, pl.ds(u * unit, unit)]
            dst = col_ref.at[
                pl.ds(pl.multiple_of(r * n + k * part, part), part), pl.ds(offset, unit)
            ]
            send = cs.at[step, h, k, u]

            @pl.when(owner != r)
            def _():
                copy = remote(src, dst, send, cr.at[r, slot, k], rows=owner)
                copy.start() if start else copy.wait_send()

            if start:
                @pl.when(owner == r)
                def _():
                    pltpu.make_async_copy(src, dst, cl.at[slot, k]).start()

    def order(h):
        return list(range(bits)) if h == 0 else list(range(bits))[::-1]

    def spread(h, stage, mask):
        bit = 1 << order(h)[stage]
        origin = r ^ (2 * mask)
        cols = pl.ds(h * half, half)
        src = x_ref.at[:, cols] if mask == 0 else all_ref.at[rows_of(origin), cols]
        return remote(
            src, all_ref.at[rows_of(origin), cols],
            ps.at[h, mask | bit], pr.at[h, mask | bit], rows=r ^ (2 * bit),
        )

    def partner(h, mask):
        origin = r ^ (2 * mask)
        cols = pl.ds(h * half, half)
        src = x_ref.at[:, cols] if mask == 0 else all_ref.at[rows_of(origin), cols]
        return remote(
            src, all_ref.at[rows_of(origin), cols],
            ds.at[h, mask], dr.at[h, mask], rows=r ^ 1,
        )

    def masks_before(h, stage):
        found = [0]
        for b in order(h)[:stage]:
            found += [m | (1 << b) for m in found]
        return found

    for k in range(SPLIT):
        for h in range(2):
            go(ring_copy(0, h, k))
    stat_local = pltpu.make_async_copy(st_ref, stat_ref.at[r, f], lsem.at[0])
    stat_local.start()
    for d in range(1, feat_count):
        go(remote(
            st_ref, stat_ref.at[r, f], ss.at[d], sr.at[d],
            feat=lax.rem(f + d, feat_count),
        ))
    for stage in range(bits):
        for h in range(2):
            go(spread(h, stage, 0))
    for h in range(2):
        go(partner(h, 0))
    own = pltpu.make_async_copy(x_ref, all_ref.at[rows_of(r)], lsem.at[1])
    own.start()
    for k in range(SPLIT):
        for h in range(2):
            column_sends(0, h, k, True)

    stat_local.wait()
    for d in range(1, feat_count):
        remote(
            st_ref, stat_ref.at[r, lax.rem(f + feat_count - d, feat_count)],
            ss.at[d], sr.at[d], feat=f,
        ).wait_recv()
    for d in range(1, row_count):
        go(remote(
            stat_ref.at[r], stat_ref.at[r], ts.at[d], tr.at[d],
            rows=lax.rem(r + d, row_count),
        ))

    def relay(stage):
        for h in range(2):
            bit = 1 << order(h)[stage]
            for m in masks_before(h, stage):
                mask = m | bit
                cols = pl.ds(h * half, half)
                remote(
                    x_ref.at[:, cols], all_ref.at[rows_of(r ^ (2 * mask)), cols],
                    ps.at[h, mask], pr.at[h, mask], rows=r,
                ).wait_recv()
                for later in range(stage + 1, bits):
                    go(spread(h, later, mask))
                go(partner(h, mask))

    for step in range(1, feat_count):
        for k in range(SPLIT):
            for h in range(2):
                ring_copy(step - 1, h, k).wait_recv()
                if step < feat_count - 1:
                    go(ring_copy(step, h, k))
                column_sends(step, h, k, True)
        if step <= bits:
            relay(step - 1)
    for stage in range(feat_count - 1, bits):
        relay(stage)

    for h in range(2):
        for mask in range(chips):
            cols = pl.ds(h * half, half)
            remote(
                x_ref.at[:, cols], all_ref.at[rows_of(r ^ (2 * mask) ^ 1), cols],
                ds.at[h, mask], dr.at[h, mask], rows=r,
            ).wait_recv()
    for d in range(1, row_count):
        origin = lax.rem(r + row_count - d, row_count)
        remote(
            stat_ref.at[origin], stat_ref.at[origin], ts.at[d], tr.at[d], rows=r
        ).wait_recv()
        for slot in range(per_owner):
            for k in range(SPLIT):
                dst = col_ref.at[
                    pl.ds(pl.multiple_of(origin * n + k * part, part), part),
                    pl.ds(slot * unit, unit),
                ]
                remote(
                    x_ref.at[pl.ds(0, part), pl.ds(0, unit)], dst,
                    cs.at[0, 0, 0, 0], cr.at[origin, slot, k], rows=r,
                ).wait_recv()
    for slot in range(per_owner):
        for k in range(SPLIT):
            dst = col_ref.at[
                pl.ds(pl.multiple_of(r * n + k * part, part), part),
                pl.ds(slot * unit, unit),
            ]
            pltpu.make_async_copy(
                x_ref.at[pl.ds(0, part), pl.ds(0, unit)], dst, cl.at[slot, k]
            ).wait()
    own.wait()
    for copy in sends:
        copy.wait_send()
    for step in range(feat_count):
        for k in range(SPLIT):
            for h in range(2):
                column_sends(step, h, k, False)


def gather(features, stats):
    row_count = lax.axis_size("rows")
    feat_count = lax.axis_size("feat")
    n, width = features.shape
    half = width // 2
    col_width = width * feat_count // row_count
    unit = min(col_width, half)
    chips = row_count // 2
    dma = pltpu.SemaphoreType.DMA
    return pl.pallas_call(
        functools.partial(gather_kernel, row_count, feat_count),
        out_shape=(
            jax.ShapeDtypeStruct((row_count * n, width), features.dtype),
            jax.ShapeDtypeStruct((row_count * n, col_width), features.dtype),
            jax.ShapeDtypeStruct((row_count, feat_count) + stats.shape, stats.dtype),
        ),
        in_specs=[pl.BlockSpec(memory_space=pltpu.VMEM)] * 2,
        out_specs=[pl.BlockSpec(memory_space=pl.ANY)] * 3,
        scratch_shapes=[
            pltpu.VMEM((feat_count - 1, n, width), features.dtype),
            dma((feat_count - 1, 2, SPLIT)), dma((feat_count - 1, 2, SPLIT)),
            dma((2, chips)), dma((2, chips)),
            dma((2, chips)), dma((2, chips)),
            dma((feat_count, 2, SPLIT, half // unit)),
            dma((row_count, col_width // unit, SPLIT)),
            dma((col_width // unit, SPLIT)),
            dma((feat_count,)), dma((feat_count,)),
            dma((row_count,)), dma((row_count,)),
            dma((2,)),
        ],
        compiler_params=pltpu.CompilerParams(
            has_side_effects=True, vmem_limit_bytes=32 * 1024 * 1024
        ),
        name="gather",
    )(features, stats)


def per_device(features, labels, posterior, prior_prec):
    row_count = lax.axis_size("rows")
    feat_count = lax.axis_size("feat")
    row_index = lax.axis_index("rows")
    feat_index = lax.axis_index("feat")
    n, block_width = features.shape
    col_width = block_width * feat_count // row_count
    partial_value = jnp.dot(features, posterior, preferred_element_type=jnp.float32)
    padded = -(-n // 512) * 512
    stats = jnp.concatenate([
        jnp.pad(partial_value, (0, padded - n)),
        jnp.pad(labels.astype(jnp.float32), (0, padded - n)),
    ]).reshape(-1, 128)
    all_rows, column_rows, all_stats = gather(features, stats)
    all_stats = all_stats.reshape(row_count, feat_count, 2, padded)[..., :n]
    margins = jnp.sum(all_stats[:, :, 0], axis=1).reshape(-1)
    all_labels = all_stats[:, 0, 1].reshape(-1)
    chance = jax.nn.sigmoid(margins)
    weight = (chance * (1.0 - chance)).astype(jnp.bfloat16)
    residual = (all_labels - chance).astype(jnp.bfloat16)
    summed = jnp.dot(residual, all_rows, preferred_element_type=jnp.float32)
    gradient = summed - prior_prec * posterior.astype(jnp.float32)
    weighted = weight[:, None] * all_rows
    product = lax.dot_general(
        weighted, column_rows, (((0,), (0,)), ((), ())), preferred_element_type=jnp.float32
    )
    global_rows = feat_index * block_width + jnp.arange(block_width, dtype=jnp.int32)
    global_cols = row_index * col_width + jnp.arange(col_width, dtype=jnp.int32)
    on_diagonal = global_rows[:, None] == global_cols[None, :]
    hessian = product + jnp.where(on_diagonal, prior_prec[:, None], jnp.float32(0.0))
    return (hessian, gradient)


def solution(mesh):
    in_specs = (P("rows", "feat"), P("rows"), P("feat"), P("feat"))
    out_specs = (P("feat", "rows"), P("feat"))
    return jax.shard_map(
        per_device, mesh=mesh, in_specs=in_specs, out_specs=out_specs, check_vma=False
    )
```

profile of v0, /device:TPU:9, one launch (start us, length us, event | category | flops | bytes accessed | tf_op | source)
XLA Modules:
  0.0 214.8 jit_solution(1005749896341196002)
XLA Ops:
  0.6 0.7 reshape.38
  1.3 1.9 fusion.3
  3.3 0.7 convert_element_type.19
  4.0 0.0 copy-start.2
  4.0 1.4 copy-done.2
  5.4 164.4 %gather.1 = (bf16[1536,4096]{1,0:T(8,128)(2,1)S(1)}, bf16[1536,2048]{1,0:T(8,128)(2,1)S(1)}, f32[8,4,8,128]{3,2,1,0:T(8,128)S(1)}) custom-call(bf16[192,4096]{1,0:T(8,128)(2,1)S(1)} %copy-done.2, f32[8,128]{1,0:T(8,128)S(1)} %pad_maximum_fusion.st_ref), custom_call_target="tpu_custom_call" | custom-call | tf_op jit(solution)/shard_map/gather/pallas_call | solution.py:221
  169.8 0.0 copy-start
  169.8 4.5 %copy-done = bf16[1536,4096]{1,0:T(8,128)(2,1)} copy-done((bf16[1536,4096]{1,0:T(8,128)(2,1)}, bf16[1536,4096]{1,0:T(8,128)(2,1)S(1)}, u32[]{:S(2)}) %copy-start) | copy-done | bytes 12582936
  174.4 0.0 copy-start.3
  174.4 2.6 %copy-done.3 = bf16[1536,2048]{1,0:T(8,128)(2,1)} copy-done((bf16[1536,2048]{1,0:T(8,128)(2,1)}, bf16[1536,2048]{1,0:T(8,128)(2,1)S(1)}, u32[]{:S(2)}) %copy-start.3) | copy-done | bytes 6291480
  176.9 0.1 reshape.37
  177.1 0.1 div.11
  177.2 0.1 reshape_squeeze.3
  177.3 0.0 copy-start.1
  177.3 35.1 %select_add_fusion = f32[4096,2048]{1,0:T(8,128)} fusion(bf16[1536,2048]{1,0:T(8,128)(2,1)} %copy-done.3, f32[4096]{0:T(1024)} %param.7, s32[2048]{0:T(1024)S(1)} %iota_add_fusion.1, s32[4096]{0:T(1024)S(1)} %iota_add_fusion, bf16[1536,4096]{1,0:T(8,128)(2,1)} %copy-done, bf16[1536]{0:T(1024)(128)(2,1)S(1)} %get-tuple-element.9), kind=kOutput, calls=%fused_computation | convolution fusion | flops 25801261056 | bytes 52472832 | tf_op jit(solution)/shard_map/dot_general | solution.py:272
  212.4 0.0 copy-start.4
  212.4 0.0 copy-start.5
  212.4 0.0 copy-done.1
  212.4 1.7 fusion.4
  214.1 0.0 copy-done.4
  214.1 0.0 copy-done.5
  214.1 0.6 multiply_subtract_fusion
  (9 shorter events, 0.1 us)
Async XLA Ops:
  4.0 1.4 copy-start.2
  169.8 4.6 %copy-start = (bf16[1536,4096]{1,0:T(8,128)(2,1)}, bf16[1536,4096]{1,0:T(8,128)(2,1)S(1)}, u32[]{:S(2)}) copy-start(bf16[1536,4096]{1,0:T(8,128)(2,1)S(1)} %get-tuple-element.6) | copy-start | bytes 37748740
  174.4 2.6 %copy-start.3 = (bf16[1536,2048]{1,0:T(8,128)(2,1)}, bf16[1536,2048]{1,0:T(8,128)(2,1)S(1)}, u32[]{:S(2)}) copy-start(bf16[1536,2048]{1,0:T(8,128)(2,1)S(1)} %get-tuple-element.7) | copy-start | bytes 18874372
  177.3 35.1 %copy-start.1 = (bf16[1536,4096]{1,0:T(8,128)(2,1)S(1)}, bf16[1536,4096]{1,0:T(8,128)(2,1)}, u32[]{:S(2)}) copy-start(bf16[1536,4096]{1,0:T(8,128)(2,1)} %copy-done) | copy-start | bytes 37748740
  212.4 1.8 copy-start.4
  212.4 1.8 copy-start.5
where the time goes:
time: 215 us
  Pallas kernels  164 us (76%)
  matrix products  38.7 us (18%)
  local copies, waits for them, and re-layouts  9.5 us (4%)
    pallas_call x1, Pallas kernels, gather(): pl.pallas_call(functools.partial(gather_kernel, row_count, feat_count), o...  164 us
    dot_general x1, matrix products, per_device(): lax.dot_general(weighted, column_rows, (((0,), (0,)), ((), ())), preferre...  35.1 us
    unnamed x13, local copies, waits for them, and re-layouts  9.25 us

commit v1 on v0

--- a/solution.py
+++ b/solution.py
@@ -9,6 +9,379 @@
 
 MESH = pl.DeviceIdType.MESH
 SPLIT = 2
+CHUNK = 16
+
+
+def line_kernel(
+    row_count, feat_count, x_ref, st_ref, all_ref, col_ref, stat_ref, abuf,
+    agr, pr, br, ar, adr, own_s, relay_s, extra_s, part_s, src_s, bf_s, af_s, ad_s,
+    ss, sr, ts, tr, lsem,
+):
+    r = lax.axis_index("rows")
+    z = lax.axis_index("feat")
+    p, c = r // 2, r % 2
+    last = feat_count - 1
+    n, width = x_ref.shape
+    half = width // 2
+    m = CHUNK
+    nch = n // m
+    avoid = jnp.where(z == 0, 0, jnp.where(z == last, last, -1))
+    relays = p != avoid
+    relays_all = (p ^ last) == avoid
+    has_down, has_up = z >= 1, z <= last - 1
+
+    def rows_of(chip, core, j):
+        return pl.ds(pl.multiple_of((chip * 2 + core) * n + j * m, m), m)
+
+    def own_rows(j):
+        return pl.ds(pl.multiple_of(j * m, m), m)
+
+    def cols_of(h):
+        return pl.ds(pl.multiple_of(h * half, half), half)
+
+    def remote(src, dst, send, recv, **where):
+        return pltpu.make_async_remote_copy(
+            src_ref=src, dst_ref=dst, send_sem=send, recv_sem=recv,
+            device_id=where, device_id_type=MESH,
+        )
+
+    def pick(q, e):
+        first = jnp.where((p ^ 1) == e, p ^ 2, p ^ 1)
+        second = jnp.where(((p ^ 1) == e) | ((p ^ 2) == e), p ^ 3, p ^ 2)
+        return jnp.where(q == 0, p, jnp.where(q == 1, first, second))
+
+    barrier = pltpu.get_barrier_semaphore()
+    for d in range(1, row_count):
+        pl.semaphore_signal(
+            barrier, inc=1, device_id={"rows": lax.rem(r + d, row_count)},
+            device_id_type=MESH,
+        )
+    for d in range(1, feat_count):
+        for other in (r, r ^ 1):
+            pl.semaphore_signal(
+                barrier, inc=1,
+                device_id={"rows": other, "feat": lax.rem(z + d, feat_count)},
+                device_id_type=MESH,
+            )
+    pl.semaphore_wait(barrier, row_count - 1 + 2 * (feat_count - 1))
+
+    stat_local = pltpu.make_async_copy(st_ref, stat_ref.at[r, z], lsem.at[0])
+    stat_local.start()
+    for d in range(1, feat_count):
+        remote(
+            st_ref, stat_ref.at[r, z], ss.at[d], sr.at[d],
+            feat=lax.rem(z + d, feat_count),
+        ).start()
+
+    def ag(dim, h, j, src, chip, rel, send):
+        remote(
+            src, all_ref.at[rows_of(chip, c, j), cols_of(h)],
+            send, agr.at[rel, h, j], rows=r ^ (2 * dim),
+        ).start()
+
+    def own_first(j, _):
+        ag(1, 0, j, x_ref.at[own_rows(j), cols_of(0)], p, 0, own_s.at[0])
+        ag(2, 1, j, x_ref.at[own_rows(j), cols_of(1)], p, 1, own_s.at[1])
+        for h in range(2):
+            src = x_ref.at[own_rows(j), cols_of(h)]
+
+            @pl.when(has_down & (p == 0))
+            def _():
+                remote(
+                    src, abuf.at[z - 1, c, own_rows(j)], own_s.at[2], ar.at[0, c, j],
+                    rows=2 * p + h, feat=z - 1,
+                ).start()
+
+            @pl.when(has_down & (p == z))
+            def _():
+                remote(
+                    src, col_ref.at[rows_of(p, c, j)], own_s.at[2], br.at[0, c, j],
+                    rows=2 * p + h, feat=z - 1,
+                ).start()
+
+            @pl.when(has_up & (p == last))
+            def _():
+                remote(
+                    src, abuf.at[z, c, own_rows(j)], own_s.at[3], ar.at[0, c, j],
+                    rows=2 * p + h, feat=z + 1,
+                ).start()
+
+            @pl.when(has_up & (p == z))
+            def _():
+                remote(
+                    src, col_ref.at[rows_of(p, c, j)], own_s.at[3], br.at[0, c, j],
+                    rows=2 * p + h, feat=z + 1,
+                ).start()
+        return 0
+
+    def own_second(j, _):
+        ag(1, 1, j, x_ref.at[own_rows(j), cols_of(1)], p, 0, own_s.at[0])
+        ag(2, 0, j, x_ref.at[own_rows(j), cols_of(0)], p, 1, own_s.at[1])
+        return 0
+
+    ahead = min(2, nch)
+    lax.fori_loop(0, ahead, own_first, 0)
+    stat_local.wait()
+    for d in range(1, feat_count):
+        remote(
+            st_ref, stat_ref.at[r, lax.rem(z + feat_count - d, feat_count)],
+            ss.at[d], sr.at[d], feat=z,
+        ).wait_recv()
+    for d in range(1, row_count):
+        remote(
+            stat_ref.at[r], stat_ref.at[r], ts.at[d], tr.at[d],
+            rows=lax.rem(r + d, row_count),
+        ).start()
+    lax.fori_loop(ahead, nch, own_first, 0)
+    lax.fori_loop(0, nch, own_second, 0)
+    own = pltpu.make_async_copy(
+        x_ref, all_ref.at[pl.ds(pl.multiple_of(r * n, n), n)], lsem.at[1]
+    )
+    own.start()
+    remote(
+        x_ref, all_ref.at[pl.ds(pl.multiple_of(r * n, n), n)], part_s.at[3], pr.at[3],
+        rows=r ^ 1,
+    ).start()
+
+    def arrive(rel, h, j):
+        chip = p ^ (rel + 1)
+        here = all_ref.at[rows_of(chip, c, j), cols_of(h)]
+        remote(here, here, own_s.at[0], agr.at[rel, h, j], rows=r).wait_recv()
+        remote(here, here, part_s.at[rel], pr.at[rel], rows=r ^ 1).start()
+
+    def forward(rel, h, j, send):
+        chip = p ^ (rel + 1)
+        here = all_ref.at[rows_of(chip, c, j), cols_of(h)]
+        ag(2 - rel, h, j, here, chip, 2, send)
+
+    def gather_event(s):
+        a, j = s // nch, s % nch
+
+        @pl.when(a == 0)
+        def _():
+            arrive(0, 0, j)
+
+            @pl.when(relays)
+            def _():
+                forward(0, 0, j, relay_s.at[0])
+            arrive(1, 1, j)
+
+            @pl.when(relays)
+            def _():
+                forward(1, 1, j, relay_s.at[1])
+
+        @pl.when(a == 1)
+        def _():
+            arrive(0, 1, j)
+
+            @pl.when(relays_all)
+            def _():
+                forward(0, 1, j, extra_s.at[0])
+            arrive(1, 0, j)
+
+            @pl.when(relays_all)
+            def _():
+                forward(1, 0, j, extra_s.at[1])
+
+        @pl.when(a == 2)
+        def _():
+            arrive(2, 0, j)
+            arrive(2, 1, j)
+
+    def source_event(s):
+        q, j = 1 + s // nch, s % nch
+        for h in range(2):
+            @pl.when(has_down)
+            def _():
+                where = rows_of(pick(q, 0), c, j)
+                remote(
+                    all_ref.at[where, cols_of(h)], col_ref.at[where],
+                    src_s.at[0, q], br.at[q, c, j], rows=2 * p + h, feat=z - 1,
+                ).start()
+
+            @pl.when(has_up)
+            def _():
+                where = rows_of(pick(q, last), c, j)
+                remote(
+                    all_ref.at[where, cols_of(h)], col_ref.at[where],
+                    src_s.at[1, q], br.at[q, c, j], rows=2 * p + h, feat=z + 1,
+                ).start()
+
+    def column_event(s):
+        q, j = s // nch, s % nch
+        down = p > z
+        chip = pick(q, jnp.where(down, 0, last))
+        for k in range(2):
+            here = col_ref.at[rows_of(chip, k, j)]
+            remote(here, here, bf_s.at[q], br.at[q, k, j], rows=r).wait_recv()
+
+            @pl.when((down & has_down) | (~down & has_up))
+            def _():
+                remote(
+                    here, here, bf_s.at[q], br.at[q, k, j],
+                    feat=jnp.where(down, z - 1, z + 1),
+                ).start()
+
+    def pass_event(s):
+        q, j = s // nch, s % nch
+        down = p == 0
+        block = jnp.where(down, z + 1 + q, z - 1 - q)
+        slot = jnp.where(down, block - 1, block)
+
+        @pl.when((block >= 0) & (block <= last))
+        def _():
+            for k in range(2):
+                here = abuf.at[slot, k, own_rows(j)]
+                remote(here, here, af_s.at[q], ar.at[q, k, j], rows=r).wait_recv()
+
+                @pl.when((down & has_down) | (~down & has_up))
+                def _():
+                    remote(
+                        here, here, af_s.at[q], ar.at[q + 1, k, j],
+                        feat=jnp.where(down, z - 1, z + 1),
+                    ).start()
+                remote(
+                    here, col_ref.at[rows_of(p, k, j)], ad_s.at[q], adr.at[0],
+                    rows=2 * block + c,
+                ).start()
+
+    items = last
+    lag = nch // 2 + 1
+
+    def step(u, _):
+        @pl.when((p != z) & (u < items * nch))
+        def _():
+            column_event(u)
+        for e in range(2):
+            s = 2 * u - 2 + e
+
+            @pl.when((s >= 0) & (s < 3 * nch))
+            def _():
+                gather_event(s)
+
+        @pl.when((p == z) & (u >= lag) & (u < lag + 2 * nch))
+        def _():
+            source_event(u - lag)
+
+        @pl.when(((p == 0) | (p == last)) & (u >= 1) & (u < 1 + items * nch))
+        def _():
+            pass_event(u - 1)
+        return 0
+
+    lax.fori_loop(0, items * nch + 1, step, 0)
+
+    for rel in range(4):
+        chip = p if rel == 3 else p ^ (rel + 1)
+        there = all_ref.at[pl.ds(pl.multiple_of((2 * chip + 1 - c) * n, n), n)]
+        remote(there, there, part_s.at[rel], pr.at[rel], rows=r).wait_recv()
+    own.wait()
+    twice = col_ref.at[pl.ds(0, 2 * n)]
+
+    @pl.when(p == z)
+    def _():
+        copy = pltpu.make_async_copy(all_ref.at[:, cols_of(c)], col_ref, lsem.at[2])
+        copy.start()
+        copy.wait()
+
+    @pl.when(p != z)
+    def _():
+        remote(twice, twice, bf_s.at[0], adr.at[0], rows=r).wait_recv()
+    for d in range(1, row_count):
+        origin = lax.rem(r + row_count - d, row_count)
+        remote(
+            stat_ref.at[origin], stat_ref.at[origin], ts.at[d], tr.at[d], rows=r
+        ).wait_recv()
+
+    def sent(ref, sem):
+        remote(ref, ref, sem, pr.at[3], rows=r).wait_send()
+
+    for d in range(1, feat_count):
+        sent(st_ref, ss.at[d])
+    for d in range(1, row_count):
+        sent(stat_ref.at[r], ts.at[d])
+    for i in range(2):
+        sent(x_ref, own_s.at[i])
+
+        @pl.when(relays)
+        def _():
+            sent(x_ref.at[:, pl.ds(0, half)], relay_s.at[i])
+
+        @pl.when(relays_all)
+        def _():
+            sent(x_ref.at[:, pl.ds(0, half)], extra_s.at[i])
+
+    @pl.when(has_down & ((p == 0) | (p == z)))
+    def _():
+        sent(x_ref, own_s.at[2])
+
+    @pl.when(has_up & ((p == last) | (p == z)))
+    def _():
+        sent(x_ref, own_s.at[3])
+    for rel in range(4):
+        sent(x_ref, part_s.at[rel])
+    down = p > z
+    for q in range(items):
+        if q > 0:
+            @pl.when((p == z) & has_down)
+            def _():
+                sent(x_ref, src_s.at[0, q])
+
+            @pl.when((p == z) & has_up)
+            def _():
+                sent(x_ref, src_s.at[1, q])
+
+        @pl.when((p != z) & ((down & has_down) | (~down & has_up)))
+        def _():
+            sent(twice, bf_s.at[q])
+        for edge, block, more in ((0, z + 1 + q, has_down), (last, z - 1 - q, has_up)):
+            @pl.when((p == edge) & (block >= 0) & (block <= last))
+            def _():
+                sent(twice, ad_s.at[q])
+
+                @pl.when(more)
+                def _():
+                    sent(twice, af_s.at[q])
+
+
+def line_gather(features, stats):
+    row_count = lax.axis_size("rows")
+    feat_count = lax.axis_size("feat")
+    n, width = features.shape
+    half = width // 2
+    items = feat_count - 1
+    nch = n // CHUNK
+    dma = pltpu.SemaphoreType.DMA
+    return pl.pallas_call(
+        functools.partial(line_kernel, row_count, feat_count),
+        out_shape=(
+            jax.ShapeDtypeStruct((row_count * n, width), features.dtype),
+            jax.ShapeDtypeStruct((row_count * n, half), features.dtype),
+            jax.ShapeDtypeStruct((row_count, feat_count) + stats.shape, stats.dtype),
+        ),
+        in_specs=[pl.BlockSpec(memory_space=pltpu.VMEM)] * 2,
+        out_specs=[pl.BlockSpec(memory_space=pl.ANY)] * 3,
+        scratch_shapes=[
+            pltpu.VMEM((items, 2, n, half), features.dtype),
+            dma((3, 2, nch)), dma((4,)), dma((items, 2, nch)), dma((items + 1, 2, nch)),
+            dma((1,)),
+            dma((4,)), dma((2,)), dma((2,)), dma((4,)), dma((2, items)), dma((items,)),
+            dma((items,)), dma((items,)),
+            dma((feat_count,)), dma((feat_count,)),
+            dma((row_count,)), dma((row_count,)),
+            dma((3,)),
+        ],
+        compiler_params=pltpu.CompilerParams(
+            collective_id=0, has_side_effects=True, vmem_limit_bytes=32 * 1024 * 1024
+        ),
+        name="line_gather",
+    )(features, stats)
+
+
+def paired(row_count, feat_count, n, width):
+    return (
+        row_count == 2 * feat_count and (feat_count - 1).bit_length() == 2
+        and feat_count & (feat_count - 1) == 0 and n % CHUNK == 0 and width % 256 == 0
+    )
 
 
 def gather_kernel(
@@ -259,7 +632,8 @@
         jnp.pad(partial_value, (0, padded - n)),
         jnp.pad(labels.astype(jnp.float32), (0, padded - n)),
     ]).reshape(-1, 128)
-    all_rows, column_rows, all_stats = gather(features, stats)
+    collect = line_gather if paired(row_count, feat_count, n, block_width) else gather
+    all_rows, column_rows, all_stats = collect(features, stats)
     all_stats = all_stats.reshape(row_count, feat_count, 2, padded)[..., :n]
     margins = jnp.sum(all_stats[:, :, 0], axis=1).reshape(-1)
     all_labels = all_stats[:, 0, 1].reshape(-1)

time: 215 us -> 177 us (0.82)
  the two profiles are of different devices: /device:TPU:9 before, /device:TPU:24 now
where the time goes in v1:
time: 177 us; the launch traced here: 176 us
  Pallas kernels  125 us (71%)
  matrix products  38.7 us (22%)
  local copies, waits for them, and re-layouts  9.5 us (5%)
    pallas_call x1, Pallas kernels, line_gather(): pl.pallas_call(functools.partial(line_kernel, row_count, feat_count), out...  125 us
    dot_general x1, matrix products, per_device(): lax.dot_general(weighted, column_rows, (((0,), (0,)), ((), ())), preferre...  35.1 us
    unnamed x13, local copies, waits for them, and re-layouts  9.25 us

profile of v1, /device:TPU:24, one launch (start us, length us, event | category | flops | bytes accessed | tf_op | source)
XLA Modules:
  0.0 175.6 jit_solution(5907892066280277199)
XLA Ops:
  0.6 0.7 reshape.38
  1.3 1.9 %fusion.3 = f32[1,192]{1,0:T(1,128)S(1)} fusion(bf16[192,4096]{1,0:T(8,128)(2,1)} %x_ref.1, bf16[4096,1]{0,1:T(2,128)(2,1)S(1)} %reshape.38), kind=kOutput, calls=%fused_computation.15 | convolution fusion | flops 1572864 | bytes 1581824 | tf_op jit(solution)/shard_map/dot_general | solution.py:629
  3.3 0.7 convert_element_type.19
  4.0 0.0 copy-start.2
  4.0 1.4 copy-done.2
  5.4 125.2 %line_gather.1 = (bf16[1536,4096]{1,0:T(8,128)(2,1)S(1)}, bf16[1536,2048]{1,0:T(8,128)(2,1)S(1)}, f32[8,4,8,128]{3,2,1,0:T(8,128)S(1)}) custom-call(bf16[192,4096]{1,0:T(8,128)(2,1)S(1)} %copy-done.2, f32[8,128]{1,0:T(8,128)S(1)} %pad_maximum_fusion.st_ref), custom_call_target="tpu_custom_call" | custom-call | tf_op jit(solution)/shard_map/line_gather/pallas_call | solution.py:354
  130.6 0.0 copy-start
  130.6 4.5 %copy-done = bf16[1536,4096]{1,0:T(8,128)(2,1)} copy-done((bf16[1536,4096]{1,0:T(8,128)(2,1)}, bf16[1536,4096]{1,0:T(8,128)(2,1)S(1)}, u32[]{:S(2)}) %copy-start) | copy-done | bytes 12582936
  135.2 0.0 copy-start.3
  135.2 2.6 %copy-done.3 = bf16[1536,2048]{1,0:T(8,128)(2,1)} copy-done((bf16[1536,2048]{1,0:T(8,128)(2,1)}, bf16[1536,2048]{1,0:T(8,128)(2,1)S(1)}, u32[]{:S(2)}) %copy-start.3) | copy-done | bytes 6291480
  137.7 0.1 reshape.37
  137.9 0.1 div.11
  138.0 0.1 reshape_squeeze.3
  138.1 0.0 copy-start.1
  138.1 35.1 %select_add_fusion = f32[4096,2048]{1,0:T(8,128)} fusion(bf16[1536,2048]{1,0:T(8,128)(2,1)} %copy-done.3, f32[4096]{0:T(1024)} %param.7, s32[2048]{0:T(1024)S(1)} %iota_add_fusion.1, s32[4096]{0:T(1024)S(1)} %iota_add_fusion, bf16[1536,4096]{1,0:T(8,128)(2,1)} %copy-done, bf16[1536]{0:T(1024)(128)(2,1)S(1)} %get-tuple-element.9), kind=kOutput, calls=%fused_computation | convolution fusion | flops 25801261056 | bytes 52472832 | tf_op jit(solution)/shard_map/dot_general | solution.py:646
  173.2 0.0 copy-start.4
  173.2 0.0 copy-start.5
  173.2 0.0 copy-done.1
  173.2 1.7 fusion.4
  174.9 0.0 copy-done.4
  174.9 0.0 copy-done.5
  174.9 0.6 multiply_subtract_fusion
  (9 shorter events, 0.1 us)
Async XLA Ops:
  4.0 1.4 copy-start.2
  130.6 4.6 %copy-start = (bf16[1536,4096]{1,0:T(8,128)(2,1)}, bf16[1536,4096]{1,0:T(8,128)(2,1)S(1)}, u32[]{:S(2)}) copy-start(bf16[1536,4096]{1,0:T(8,128)(2,1)S(1)} %get-tuple-element.6) | copy-start | bytes 37748740
  135.2 2.6 %copy-start.3 = (bf16[1536,2048]{1,0:T(8,128)(2,1)}, bf16[1536,2048]{1,0:T(8,128)(2,1)S(1)}, u32[]{:S(2)}) copy-start(bf16[1536,2048]{1,0:T(8,128)(2,1)S(1)} %get-tuple-element.7) | copy-start | bytes 18874372
  138.1 35.1 %copy-start.1 = (bf16[1536,4096]{1,0:T(8,128)(2,1)S(1)}, bf16[1536,4096]{1,0:T(8,128)(2,1)}, u32[]{:S(2)}) copy-start(bf16[1536,4096]{1,0:T(8,128)(2,1)} %copy-done) | copy-start | bytes 37748740
  173.2 1.8 %copy-start.4 = (bf16[4096]{0:T(1024)(128)(2,1)S(1)}, bf16[4096]{0:T(1024)(128)(2,1)}, u32[]{:S(2)}) copy-start(bf16[4096]{0:T(1024)(128)(2,1)} %param.6) | copy-start | bytes 24580
  173.2 1.8 %copy-start.5 = (f32[4096]{0:T(1024)S(1)}, f32[4096]{0:T(1024)}, u32[]{:S(2)}) copy-start(f32[4096]{0:T(1024)} %param.7) | copy-start | bytes 49156

commit v2 on v1

--- a/solution.py
+++ b/solution.py
@@ -10,10 +10,45 @@
 MESH = pl.DeviceIdType.MESH
 SPLIT = 2
 CHUNK = 16
+TILE = 512
+AHEAD = 3
+VMEM_BUDGET = 60 * 1024 * 1024
+
+
+def pick(p, q, e):
+    first = jnp.where((p ^ 1) == e, p ^ 2, p ^ 1)
+    second = jnp.where(((p ^ 1) == e) | ((p ^ 2) == e), p ^ 3, p ^ 2)
+    return jnp.where(q == 0, p, jnp.where(q == 1, first, second))
+
+
+def passed_chip(p, z, last):
+    return jnp.where(p > z, 0, jnp.where(p < z, last, p ^ 3))
+
+
+def slabs(ref, lead, starts, size, cols):
+    parts = []
+    for start in starts:
+        rows = pl.ds(pl.multiple_of(start, CHUNK), size)
+        parts.append(ref[rows, cols] if lead is None else ref[lead, rows, cols])
+    return jnp.concatenate(parts, axis=0)
+
+
+def wide(value, width):
+    return jnp.concatenate([value] * (width // value.shape[1]), axis=1)
+
+
+def weigh(all_ref, wr_ref, gacc_ref, starts, size, cols, width):
+    x = slabs(all_ref, None, starts, size, cols)
+    weight = slabs(wr_ref, 0, starts, size, slice(None))
+    residual = slabs(wr_ref, 1, starts, size, slice(None)).astype(jnp.float32)
+    pulled = x.astype(jnp.float32) * wide(residual, width)
+    pulled = jnp.sum(pulled.reshape(-1, 8, width), axis=0)
+    return x * wide(weight, width), gacc_ref[:, cols] + pulled
 
 
 def line_kernel(
-    row_count, feat_count, x_ref, st_ref, all_ref, col_ref, stat_ref, abuf,
+    row_count, feat_count, x_ref, st_ref, prec_ref,
+    h_ref, all_ref, col_ref, wr_ref, gacc_ref, abuf, stat_ref,
     agr, pr, br, ar, adr, own_s, relay_s, extra_s, part_s, src_s, bf_s, af_s, ad_s,
     ss, sr, ts, tr, lsem,
 ):
@@ -45,11 +80,6 @@
             device_id=where, device_id_type=MESH,
         )
 
-    def pick(q, e):
-        first = jnp.where((p ^ 1) == e, p ^ 2, p ^ 1)
-        second = jnp.where(((p ^ 1) == e) | ((p ^ 2) == e), p ^ 3, p ^ 2)
-        return jnp.where(q == 0, p, jnp.where(q == 1, first, second))
-
     barrier = pltpu.get_barrier_semaphore()
     for d in range(1, row_count):
         pl.semaphore_signal(
@@ -79,9 +109,20 @@
             send, agr.at[rel, h, j], rows=r ^ (2 * dim),
         ).start()
 
-    def own_first(j, _):
-        ag(1, 0, j, x_ref.at[own_rows(j), cols_of(0)], p, 0, own_s.at[0])
-        ag(2, 1, j, x_ref.at[own_rows(j), cols_of(1)], p, 1, own_s.at[1])
+    def own_plane(s):
+        j = lax.rem(s, nch)
+
+        @pl.when(s < nch)
+        def _():
+            ag(1, 0, j, x_ref.at[own_rows(j), cols_of(0)], p, 0, own_s.at[0])
+            ag(2, 1, j, x_ref.at[own_rows(j), cols_of(1)], p, 1, own_s.at[1])
+
+        @pl.when(s >= nch)
+        def _():
+            ag(1, 1, j, x_ref.at[own_rows(j), cols_of(1)], p, 0, own_s.at[0])
+            ag(2, 0, j, x_ref.at[own_rows(j), cols_of(0)], p, 1, own_s.at[1])
+
+    def own_line(j):
         for h in range(2):
             src = x_ref.at[own_rows(j), cols_of(h)]
 
@@ -112,37 +153,62 @@
                     src, col_ref.at[rows_of(p, c, j)], own_s.at[3], br.at[0, c, j],
                     rows=2 * p + h, feat=z + 1,
                 ).start()
+
+    def own_sends(j, _):
+        own_plane(2 * j)
+        own_plane(2 * j + 1)
+        own_line(j)
         return 0
 
-    def own_second(j, _):
-        ag(1, 1, j, x_ref.at[own_rows(j), cols_of(1)], p, 0, own_s.at[0])
-        ag(2, 0, j, x_ref.at[own_rows(j), cols_of(0)], p, 1, own_s.at[1])
-        return 0
-
-    ahead = min(2, nch)
-    lax.fori_loop(0, ahead, own_first, 0)
-    stat_local.wait()
-    for d in range(1, feat_count):
-        remote(
-            st_ref, stat_ref.at[r, lax.rem(z + feat_count - d, feat_count)],
-            ss.at[d], sr.at[d], feat=z,
-        ).wait_recv()
-    for d in range(1, row_count):
-        remote(
-            stat_ref.at[r], stat_ref.at[r], ts.at[d], tr.at[d],
-            rows=lax.rem(r + d, row_count),
-        ).start()
-    lax.fori_loop(ahead, nch, own_first, 0)
-    lax.fori_loop(0, nch, own_second, 0)
     own = pltpu.make_async_copy(
         x_ref, all_ref.at[pl.ds(pl.multiple_of(r * n, n), n)], lsem.at[1]
     )
+    lax.fori_loop(0, AHEAD, own_sends, 0)
     own.start()
     remote(
         x_ref, all_ref.at[pl.ds(pl.multiple_of(r * n, n), n)], part_s.at[3], pr.at[3],
         rows=r ^ 1,
     ).start()
 
+    def share_stats():
+        stat_local.wait()
+        for d in range(1, feat_count):
+            remote(
+                st_ref, stat_ref.at[r, lax.rem(z + feat_count - d, feat_count)],
+                ss.at[d], sr.at[d], feat=z,
+            ).wait_recv()
+        for d in range(1, row_count):
+            remote(
+                stat_ref.at[r], stat_ref.at[r], ts.at[d], tr.at[d],
+                rows=lax.rem(r + d, row_count),
+            ).start()
+
+    def weights():
+        for d in range(1, row_count):
+            origin = lax.rem(r + row_count - d, row_count)
+            remote(
+                stat_ref.at[origin], stat_ref.at[origin], ts.at[d], tr.at[d], rows=r
+            ).wait_recv()
+
+        def one(i, _):
+            margins = stat_ref[i, 0, 0:8]
+            for f in range(1, feat_count):
+                margins = margins + stat_ref[i, f, 0:8]
+            chance = 1.0 / (1.0 + jnp.exp(-margins))
+            weight = (chance * (1.0 - chance)).astype(jnp.bfloat16)
+            residual = (stat_ref[i, 0, 8:16] - chance).astype(jnp.bfloat16)
+            for lead, value in ((0, weight), (1, residual)):
+                turned = value.astype(jnp.float32).T
+                for t in range(-(-n // 128)):
+                    count = min(128, n - 128 * t)
+                    rows = pl.ds(pl.multiple_of(i * n + 128 * t, CHUNK), count)
+                    wr_ref[lead, rows, :] = jnp.broadcast_to(
+                        turned[:count, t:t + 1], (count, 128)
+                    ).astype(jnp.bfloat16)
+            return 0
+
+        lax.fori_loop(0, row_count, one, 0)
+
     def arrive(rel, h, j):
         chip = p ^ (rel + 1)
         here = all_ref.at[rows_of(chip, c, j), cols_of(h)]
@@ -193,7 +259,7 @@
         for h in range(2):
             @pl.when(has_down)
             def _():
-                where = rows_of(pick(q, 0), c, j)
+                where = rows_of(pick(p, q, 0), c, j)
                 remote(
                     all_ref.at[where, cols_of(h)], col_ref.at[where],
                     src_s.at[0, q], br.at[q, c, j], rows=2 * p + h, feat=z - 1,
@@ -201,7 +267,7 @@
 
             @pl.when(has_up)
             def _():
-                where = rows_of(pick(q, last), c, j)
+                where = rows_of(pick(p, q, last), c, j)
                 remote(
                     all_ref.at[where, cols_of(h)], col_ref.at[where],
                     src_s.at[1, q], br.at[q, c, j], rows=2 * p + h, feat=z + 1,
@@ -210,7 +276,7 @@
     def column_event(s):
         q, j = s // nch, s % nch
         down = p > z
-        chip = pick(q, jnp.where(down, 0, last))
+        chip = pick(p, q, jnp.where(down, 0, last))
         for k in range(2):
             here = col_ref.at[rows_of(chip, k, j)]
             remote(here, here, bf_s.at[q], br.at[q, k, j], rows=r).wait_recv()
@@ -241,17 +307,117 @@
                         feat=jnp.where(down, z - 1, z + 1),
                     ).start()
                 remote(
-                    here, col_ref.at[rows_of(p, k, j)], ad_s.at[q], adr.at[0],
+                    here, col_ref.at[rows_of(p, k, j)], ad_s.at[q], adr.at[j // (nch // 2)],
                     rows=2 * block + c,
                 ).start()
 
     items = last
     lag = nch // 2 + 1
+    tiles = width // TILE
+    edge = passed_chip(p, z, last)
+    twice = col_ref.at[pl.ds(0, 2 * n)]
+    once = col_ref.at[pl.ds(0, n)]
+    hn = n // 2
+    q = nch // 6
+    starts = [4 * q, 6 * q, 9 * q, 12 * q, 15 * q, 33 * q // 2]
+    stops = [6 * q, 8 * q, 11 * q, 14 * q, 33 * q // 2, 18 * q]
+
+    def partner_rows(chip):
+        rel = jnp.where(chip == p, 3, (p ^ chip) - 1)
+        there = all_ref.at[pl.ds(pl.multiple_of((2 * chip + 1 - c) * n, n), n)]
+        remote(there, there, part_s.at[rel], pr.at[rel], rows=r).wait_recv()
+
+        @pl.when(p == z)
+        def _():
+            rows = pl.ds(pl.multiple_of(chip * 2 * n, n), 2 * n)
+            copy = pltpu.make_async_copy(
+                all_ref.at[rows, cols_of(c)], col_ref.at[rows], lsem.at[2]
+            )
+            copy.start()
+            copy.wait()
+
+    def prepare(i):
+        rows = pl.ds(pl.multiple_of(i * TILE, TILE), TILE)
+        h_ref[rows, :] = jnp.zeros((TILE, half), jnp.float32)
+        offset = i * TILE - c * half
+
+        @pl.when((p == z) & (offset >= 0) & (offset < half))
+        def _():
+            cols = pl.ds(pl.multiple_of(offset, TILE), TILE)
+            shape = (TILE, TILE)
+            same = lax.broadcasted_iota(jnp.int32, shape, 0) == lax.broadcasted_iota(
+                jnp.int32, shape, 1
+            )
+            h_ref[rows, cols] = jnp.where(
+                same, jnp.broadcast_to(prec_ref[:, rows], shape), 0.0
+            )
+
+    def unit(index):
+        chip = jnp.where(
+            index < 2, p,
+            jnp.where(index < 4, pick(p, 1, edge), jnp.where(index == 4, pick(p, 2, edge), edge)),
+        )
+        piece = jnp.where((index == 1) | (index == 3), 1, 0)
+        return chip, piece
+
+    def multiply(chip, piece, i):
+        cols = pl.ds(pl.multiple_of(i * TILE, TILE), TILE)
+        first = [(chip * 2 + k) * n + piece * hn for k in range(2)]
+        weighted, pulled = weigh(all_ref, wr_ref, gacc_ref, first, hn, cols, TILE)
+        gacc_ref[:, cols] = pulled
+        turned = weighted.T
+        for t in range(half // TILE):
+            there = pl.ds(t * TILE, TILE)
+            h_ref[cols, there] += jnp.dot(
+                turned, slabs(col_ref, None, first, hn, there),
+                preferred_element_type=jnp.float32,
+            )
+
+    def compute(u):
+        index = sum((u >= s).astype(jnp.int32) for s in starts) - 1
+
+        def choose(values):
+            out = values[0]
+            for i in range(1, len(values)):
+                out = jnp.where(index >= i, values[i], out)
+            return out
+
+        begin, end = choose(starts), choose(stops)
+        speed = choose([-(-tiles // (e - s)) for s, e in zip(starts, stops)])
+        low = jnp.minimum((u - begin) * speed, tiles)
+        high = jnp.minimum(low + speed, tiles)
+        chip, piece = unit(index)
+
+        @pl.when(u == begin)
+        def _():
+            @pl.when(index == 0)
+            def _():
+                own.wait()
+                weights()
+                gacc_ref[...] = jnp.zeros_like(gacc_ref)
+
+            @pl.when((index != 1) & (index != 3))
+            def _():
+                partner_rows(chip)
+
+            @pl.when((index == 5) & (p != z))
+            def _():
+                remote(once, once, bf_s.at[0], adr.at[0], rows=r).wait_recv()
+
+        def one(i, _):
+            multiply(chip, piece, i)
+            return 0
+
+        lax.fori_loop(low, high, one, 0)
 
     def step(u, _):
         @pl.when((p != z) & (u < items * nch))
         def _():
             column_event(u)
+
+        @pl.when(u + AHEAD < nch)
+        def _():
+            own_sends(u + AHEAD, 0)
         for e in range(2):
             s = 2 * u - 2 + e
 
@@ -266,31 +432,31 @@
         @pl.when(((p == 0) | (p == last)) & (u >= 1) & (u < 1 + items * nch))
         def _():
             pass_event(u - 1)
+
+        @pl.when(u == 3)
+        def _():
+            share_stats()
+
+        @pl.when(u < starts[0])
+        def _():
+            def some(i, _):
+                prepare(i)
+                return 0
+            per = -(-tiles // starts[0])
+            lax.fori_loop(
+                jnp.minimum(u * per, tiles), jnp.minimum(u * per + per, tiles), some, 0
+            )
+
+        @pl.when(u >= starts[0])
+        def _():
+            compute(u)
         return 0
 
     lax.fori_loop(0, items * nch + 1, step, 0)
-
-    for rel in range(4):
-        chip = p if rel == 3 else p ^ (rel + 1)
-        there = all_ref.at[pl.ds(pl.multiple_of((2 * chip + 1 - c) * n, n), n)]
-        remote(there, there, part_s.at[rel], pr.at[rel], rows=r).wait_recv()
-    own.wait()
-    twice = col_ref.at[pl.ds(0, 2 * n)]
-
-    @pl.when(p == z)
-    def _():
-        copy = pltpu.make_async_copy(all_ref.at[:, cols_of(c)], col_ref, lsem.at[2])
-        copy.start()
-        copy.wait()
 
     @pl.when(p != z)
     def _():
-        remote(twice, twice, bf_s.at[0], adr.at[0], rows=r).wait_recv()
-    for d in range(1, row_count):
-        origin = lax.rem(r + row_count - d, row_count)
-        remote(
-            stat_ref.at[origin], stat_ref.at[origin], ts.at[d], tr.at[d], rows=r
-        ).wait_recv()
+        remote(once, once, bf_s.at[0], adr.at[1], rows=r).wait_recv()
 
     def sent(ref, sem):
         remote(ref, ref, sem, pr.at[3], rows=r).wait_send()
@@ -343,7 +509,7 @@
                     sent(twice, af_s.at[q])
 
 
-def line_gather(features, stats):
+def line_stage(features, stats, prec):
     row_count = lax.axis_size("rows")
     feat_count = lax.axis_size("feat")
     n, width = features.shape
@@ -354,16 +520,22 @@
     return pl.pallas_call(
         functools.partial(line_kernel, row_count, feat_count),
         out_shape=(
-            jax.ShapeDtypeStruct((row_count * n, width), features.dtype),
-            jax.ShapeDtypeStruct((row_count * n, half), features.dtype),
-            jax.ShapeDtypeStruct((row_count, feat_count) + stats.shape, stats.dtype),
+            pltpu.VMEM((width, half), jnp.float32),
+            pltpu.VMEM((row_count * n, width), features.dtype),
+            pltpu.VMEM((row_count * n, half), features.dtype),
+            pltpu.VMEM((2, row_count * n, 128), features.dtype),
+            pltpu.VMEM((8, width), jnp.float32),
         ),
-        in_specs=[pl.BlockSpec(memory_space=pltpu.VMEM)] * 2,
-        out_specs=[pl.BlockSpec(memory_space=pl.ANY)] * 3,
+        in_specs=[
+            pl.BlockSpec(memory_space=pl.ANY), pl.BlockSpec(memory_space=pltpu.VMEM),
+            pl.BlockSpec(memory_space=pltpu.VMEM),
+        ],
+        out_specs=[pl.BlockSpec(memory_space=pltpu.VMEM)] * 5,
         scratch_shapes=[
             pltpu.VMEM((items, 2, n, half), features.dtype),
+            pltpu.VMEM((row_count, feat_count) + stats.shape, stats.dtype),
             dma((3, 2, nch)), dma((4,)), dma((items, 2, nch)), dma((items + 1, 2, nch)),
-            dma((1,)),
+            dma((2,)),
             dma((4,)), dma((2,)), dma((2,)), dma((4,)), dma((2, items)), dma((items,)),
             dma((items,)), dma((items,)),
             dma((feat_count,)), dma((feat_count,)),
@@ -371,17 +543,107 @@
             dma((3,)),
         ],
         compiler_params=pltpu.CompilerParams(
-            collective_id=0, has_side_effects=True, vmem_limit_bytes=32 * 1024 * 1024
+            collective_id=0, has_side_effects=True, vmem_limit_bytes=10 * 1024 * 1024
         ),
-        name="line_gather",
-    )(features, stats)
+        name="line_stage",
+    )(features, stats, prec)
+
+
+def last_kernel(
+    row_count, feat_count, h_ref, all_ref, col_ref, wr_ref, gacc_ref, pull_ref,
+    out_ref, grad_ref, stage, ycols, total, sem,
+):
+    r = lax.axis_index("rows")
+    z = lax.axis_index("feat")
+    p, c = r // 2, r % 2
+    last = feat_count - 1
+    edge = passed_chip(p, z, last)
+    width, half = h_ref.shape
+    n = all_ref.shape[0] // row_count
+    hn = n // 2
+    first = [
+        (chip * 2 + k) * n + hn for chip in (edge, pick(p, 2, edge)) for k in range(2)
+    ]
+    slots, tile = stage.shape[:2]
+    for i, start in enumerate(first):
+        ycols[pl.ds(i * hn, hn), :] = col_ref[pl.ds(pl.multiple_of(start, CHUNK), hn), :]
+
+    def put(i, slot):
+        rows = pl.ds(pl.multiple_of(i * tile, tile), tile)
+        return pltpu.make_async_copy(stage.at[slot], out_ref.at[rows], sem.at[slot])
+
+    def one(i, _):
+        slot = lax.rem(i, slots)
+
+        @pl.when(i >= slots)
+        def _():
+            put(i - slots, slot).wait()
+        cols = pl.ds(pl.multiple_of(i * tile, tile), tile)
+        weighted, pulled = weigh(all_ref, wr_ref, gacc_ref, first, hn, cols, tile)
+        grad_ref[:, cols] = jnp.sum(pulled, axis=0, keepdims=True) - pull_ref[:, cols]
+        turned = weighted.T
+        for t in range(half // TILE):
+            there = pl.ds(t * TILE, TILE)
+            stage[slot, :, there] = h_ref[cols, there] + jnp.dot(
+                turned, ycols[:, there], preferred_element_type=jnp.float32
+            )
+        put(i, slot).start()
+        return 0
+
+    count = width // tile
+    lax.fori_loop(0, count, one, 0)
+    for i in range(max(0, count - slots), count):
+        put(i, i % slots).wait()
+
+
+def last_stage(h, all_rows, col_rows, wr, gacc, pull):
+    row_count = lax.axis_size("rows")
+    feat_count = lax.axis_size("feat")
+    width, half = h.shape
+    n = all_rows.shape[0] // row_count
+    return pl.pallas_call(
+        functools.partial(last_kernel, row_count, feat_count),
+        out_shape=(
+            jax.ShapeDtypeStruct((width, half), jnp.float32),
+            jax.ShapeDtypeStruct((1, width), jnp.float32),
+        ),
+        in_specs=[pl.BlockSpec(memory_space=pltpu.VMEM)] * 6,
+        out_specs=[
+            pl.BlockSpec(memory_space=pl.ANY), pl.BlockSpec(memory_space=pltpu.VMEM),
+        ],
+        scratch_shapes=[
+            pltpu.VMEM((2, 256, half), jnp.float32),
+            pltpu.VMEM((2 * n, half), all_rows.dtype),
+            pltpu.VMEM((8, 128), jnp.float32),
+            pltpu.SemaphoreType.DMA((2,)),
+        ],
+        compiler_params=pltpu.CompilerParams(vmem_limit_bytes=9 * 1024 * 1024),
+        name="last_stage",
+    )(*[pltpu.with_memory_space_constraint(a, pltpu.VMEM) for a in (h, all_rows, col_rows, wr, gacc)], pull)
 
 
 def paired(row_count, feat_count, n, width):
+    half = width // 2
+    rows = row_count * n
+    held = 4 * width * half + 2 * rows * (width + half) + 12 * n * half
     return (
         row_count == 2 * feat_count and (feat_count - 1).bit_length() == 2
-        and feat_count & (feat_count - 1) == 0 and n % CHUNK == 0 and width % 256 == 0
+        and feat_count & (feat_count - 1) == 0 and n % (6 * CHUNK) == 0
+        and n <= 1024 and half % TILE == 0 and held <= VMEM_BUDGET
     )
+
+
+def by_lines(features, labels, posterior, prior_prec):
+    n, width = features.shape
+    partial_value = jnp.dot(features, posterior, preferred_element_type=jnp.float32)
+    stats = jnp.stack([
+        jnp.pad(partial_value, (0, 1024 - n)),
+        jnp.pad(labels.astype(jnp.float32), (0, 1024 - n)),
+    ]).reshape(-1, 128)
+    pull = (prior_prec * posterior.astype(jnp.float32)).reshape(1, width)
+    held = line_stage(features, stats, prior_prec.reshape(1, width))
+    hessian, gradient = last_stage(*held, pull)
+    return (hessian, gradient.reshape(width))
 
 
 def gather_kernel(
@@ -625,6 +887,8 @@
     row_index = lax.axis_index("rows")
     feat_index = lax.axis_index("feat")
     n, block_width = features.shape
+    if paired(row_count, feat_count, n, block_width):
+        return by_lines(features, labels, posterior, prior_prec)
     col_width = block_width * feat_count // row_count
     partial_value = jnp.dot(features, posterior, preferred_element_type=jnp.float32)
     padded = -(-n // 512) * 512
@@ -632,8 +896,7 @@
         jnp.pad(partial_value, (0, padded - n)),
         jnp.pad(labels.astype(jnp.float32), (0, padded - n)),
     ]).reshape(-1, 128)
-    collect = line_gather if paired(row_count, feat_count, n, block_width) else gather
-    all_rows, column_rows, all_stats = collect(features, stats)
+    all_rows, column_rows, all_stats = gather(features, stats)
     all_stats = all_stats.reshape(row_count, feat_count, 2, padded)[..., :n]
     margins = jnp.sum(all_stats[:, :, 0], axis=1).reshape(-1)
     all_labels = all_stats[:, 0, 1].reshape(-1)

time: 177 us -> 217 us (1.23)
  Pallas kernels: 125 us -> 174 us
  matrix products: 38.7 us -> 1.92 us
  local copies, waits for them, and re-layouts: 9.5 us -> 38 us
    pallas_call x1 -> x2, Pallas kernels: 125 us -> 174 us  [the longest x1 155 us: line_stage(): pl.pallas_call(functools.partial(line_kernel, row_count, feat_count), out...]
    dot_general x3 -> x1, matrix products: 38.7 us -> 1.92 us  [by_lines(): jnp.dot(features, posterior, preferred_element_type=jnp.float32)]
    unnamed x13, local copies, waits for them, and re-layouts: 9.25 us -> 37.4 us
where the time goes in v2:
time: 217 us
  Pallas kernels  174 us (80%)
  local copies, waits for them, and re-layouts  38 us (18%)
    pallas_call x1, Pallas kernels, line_stage(): pl.pallas_call(functools.partial(line_kernel, row_count, feat_count), out...  155 us
    unnamed x13, local copies, waits for them, and re-layouts  37.4 us
    pallas_call x1, Pallas kernels, last_stage(): pl.pallas_call(functools.partial(last_kernel, row_count, feat_count), out...  18.8 us

profile of v2, /device:TPU:24, one launch (start us, length us, event | category | flops | bytes accessed | tf_op | source)
XLA Modules:
  0.0 216.6 jit_solution(7843536784647146227)
XLA Ops:
  0.6 0.7 convert_element_type.9
  1.3 1.3 convert_multiply_fusion
  2.6 0.7 reshape.20
  3.3 1.9 fusion
  5.3 0.6 reshape.16.st_ref
  5.9 155.2 %line_stage.1 = (f32[4096,2048]{1,0:T(8,128)S(1)}, bf16[1536,4096]{1,0:T(8,128)(2,1)S(1)}, bf16[1536,2048]{1,0:T(8,128)(2,1)S(1)}, bf16[2,1536,128]{2,1,0:T(8,128)(2,1)S(1)}, f32[8,4096]{1,0:T(8,128)S(1)}) custom-call(bf16[192,4096]{1,0:T(8,128)(2,1)} %x_ref.1, f32[16,128]{1,0:T(8,128)} %reshape.16.st_ref, f32[1,4096]{1,0:T(1,128)} %bitcast.8), custom_call_target="tpu_custom_call" | custom-call | tf_op jit(solution)/shard_map/line_stage/pallas_call | solution.py:520
  161.1 0.0 copy-start
  161.1 11.7 %copy-done = f32[4096,2048]{1,0:T(8,128)} copy-done((f32[4096,2048]{1,0:T(8,128)}, f32[4096,2048]{1,0:T(8,128)S(1)}, u32[]{:S(2)}) %copy-start) | copy-done | bytes 33554456
  172.8 0.0 copy-start.2
  172.8 4.5 %copy-done.2 = bf16[1536,4096]{1,0:T(8,128)(2,1)} copy-done((bf16[1536,4096]{1,0:T(8,128)(2,1)}, bf16[1536,4096]{1,0:T(8,128)(2,1)S(1)}, u32[]{:S(2)}) %copy-start.2) | copy-done | bytes 12582936
  177.3 0.0 copy-start.4
  177.3 2.6 %copy-done.4 = bf16[1536,2048]{1,0:T(8,128)(2,1)} copy-done((bf16[1536,2048]{1,0:T(8,128)(2,1)}, bf16[1536,2048]{1,0:T(8,128)(2,1)S(1)}, u32[]{:S(2)}) %copy-start.4) | copy-done | bytes 6291480
  179.9 0.0 copy-start.1
  179.9 10.5 %copy-done.1 = f32[4096,2048]{1,0:T(8,128)S(1)} copy-done((f32[4096,2048]{1,0:T(8,128)S(1)}, f32[4096,2048]{1,0:T(8,128)}, u32[]{:S(2)}) %copy-start.1) | copy-done | bytes 33554456
  190.5 0.0 copy-start.3
  190.5 4.6 %copy-done.3 = bf16[1536,4096]{1,0:T(8,128)(2,1)S(1)} copy-done((bf16[1536,4096]{1,0:T(8,128)(2,1)S(1)}, bf16[1536,4096]{1,0:T(8,128)(2,1)}, u32[]{:S(2)}) %copy-start.3) | copy-done | bytes 12582936
  195.1 0.0 copy-start.5
  195.1 2.8 %copy-done.5 = bf16[1536,2048]{1,0:T(8,128)(2,1)S(1)} copy-done((bf16[1536,2048]{1,0:T(8,128)(2,1)S(1)}, bf16[1536,2048]{1,0:T(8,128)(2,1)}, u32[]{:S(2)}) %copy-start.5) | copy-done | bytes 6291480
  197.8 18.8 %last_stage.1 = (f32[4096,2048]{1,0:T(8,128)}, f32[1,4096]{1,0:T(1,128)}) custom-call(f32[4096,2048]{1,0:T(8,128)S(1)} %copy-done.1, bf16[1536,4096]{1,0:T(8,128)(2,1)S(1)} %copy-done.3, bf16[1536,2048]{1,0:T(8,128)(2,1)S(1)} %copy-done.5, bf16[2,1536,128]{2,1,0:T(8,128)(2,1)S(1)} %get-tuple-element.12.wr_ref, f32[8,4096]{1,0:T(8,128)S(1)} %get-tuple-element.13.gacc_ref, ...), custom_call_target="tpu_custom_call" | custom-call | tf_op jit(solution)/shard_map/last_stage/pallas_call | solution.py:604
  (3 shorter events, 0.0 us)
Async XLA Ops:
  161.1 11.7 %copy-start = (f32[4096,2048]{1,0:T(8,128)}, f32[4096,2048]{1,0:T(8,128)S(1)}, u32[]{:S(2)}) copy-start(f32[4096,2048]{1,0:T(8,128)S(1)} %get-tuple-element.9.h_ref) | copy-start | bytes 100663296
  172.8 4.5 %copy-start.2 = (bf16[1536,4096]{1,0:T(8,128)(2,1)}, bf16[1536,4096]{1,0:T(8,128)(2,1)S(1)}, u32[]{:S(2)}) copy-start(bf16[1536,4096]{1,0:T(8,128)(2,1)S(1)} %get-tuple-element.10.all_ref) | copy-start | bytes 37748740
  177.3 2.6 %copy-start.4 = (bf16[1536,2048]{1,0:T(8,128)(2,1)}, bf16[1536,2048]{1,0:T(8,128)(2,1)S(1)}, u32[]{:S(2)}) copy-start(bf16[1536,2048]{1,0:T(8,128)(2,1)S(1)} %get-tuple-element.11.col_ref) | copy-start | bytes 18874372
  179.9 10.5 %copy-start.1 = (f32[4096,2048]{1,0:T(8,128)S(1)}, f32[4096,2048]{1,0:T(8,128)}, u32[]{:S(2)}) copy-start(f32[4096,2048]{1,0:T(8,128)} %copy-done) | copy-start | bytes 100663296
  190.5 4.6 %copy-start.3 = (bf16[1536,4096]{1,0:T(8,128)(2,1)S(1)}, bf16[1536,4096]{1,0:T(8,128)(2,1)}, u32[]{:S(2)}) copy-start(bf16[1536,4096]{1,0:T(8,128)(2,1)} %copy-done.2) | copy-start | bytes 37748740
  195.1 2.8 %copy-start.5 = (bf16[1536,2048]{1,0:T(8,128)(2,1)S(1)}, bf16[1536,2048]{1,0:T(8,128)(2,1)}, u32[]{:S(2)}) copy-start(bf16[1536,2048]{1,0:T(8,128)(2,1)} %copy-done.4) | copy-start | bytes 18874372

commit v3 on v2

--- a/solution.py
+++ b/solution.py
@@ -11,6 +11,7 @@
 SPLIT = 2
 CHUNK = 16
 TILE = 512
+PART = 256
 AHEAD = 3
 VMEM_BUDGET = 60 * 1024 * 1024
 
@@ -37,18 +38,19 @@
     return jnp.concatenate([value] * (width // value.shape[1]), axis=1)
 
 
-def weigh(all_ref, wr_ref, gacc_ref, starts, size, cols, width):
+def weigh(all_ref, wr_ref, starts, size, cols):
     x = slabs(all_ref, None, starts, size, cols)
     weight = slabs(wr_ref, 0, starts, size, slice(None))
     residual = slabs(wr_ref, 1, starts, size, slice(None)).astype(jnp.float32)
-    pulled = x.astype(jnp.float32) * wide(residual, width)
-    pulled = jnp.sum(pulled.reshape(-1, 8, width), axis=0)
-    return x * wide(weight, width), gacc_ref[:, cols] + pulled
+    pulled = x.astype(jnp.float32) * wide(residual, PART)
+    pulled = jnp.sum(pulled.reshape(-1, 8, PART), axis=0)
+    return (x * wide(weight, PART)).T, pulled
 
 
 def line_kernel(
     row_count, feat_count, x_ref, st_ref, prec_ref,
-    h_ref, all_ref, col_ref, wr_ref, gacc_ref, abuf, stat_ref,
+    h_ref, turned_out, cols_out, pull_out,
+    all_ref, col_ref, wr_ref, gacc_ref, kept, even, odd, abuf, stat_ref,
     agr, pr, br, ar, adr, own_s, relay_s, extra_s, part_s, src_s, bf_s, af_s, ad_s,
     ss, sr, ts, tr, lsem,
 ):
@@ -319,8 +321,9 @@
     once = col_ref.at[pl.ds(0, n)]
     hn = n // 2
     q = nch // 6
-    starts = [4 * q, 6 * q, 9 * q, 12 * q, 15 * q, 33 * q // 2]
-    stops = [6 * q, 8 * q, 11 * q, 14 * q, 33 * q // 2, 18 * q]
+    begins = [6 * q, 10 * q, 12 * q, 15 * q]
+    ends = [10 * q, 12 * q, 15 * q, 18 * q]
+    near, far = pick(p, 1, edge), pick(p, 2, edge)
 
     def partner_rows(chip):
         rel = jnp.where(chip == p, 3, (p ^ chip) - 1)
@@ -352,29 +355,35 @@
                 same, jnp.broadcast_to(prec_ref[:, rows], shape), 0.0
             )
 
-    def unit(index):
-        chip = jnp.where(
-            index < 2, p,
-            jnp.where(index < 4, pick(p, 1, edge), jnp.where(index == 4, pick(p, 2, edge), edge)),
-        )
-        piece = jnp.where((index == 1) | (index == 3), 1, 0)
-        return chip, piece
-
-    def multiply(chip, piece, i):
-        cols = pl.ds(pl.multiple_of(i * TILE, TILE), TILE)
-        first = [(chip * 2 + k) * n + piece * hn for k in range(2)]
-        weighted, pulled = weigh(all_ref, wr_ref, gacc_ref, first, hn, cols, TILE)
-        gacc_ref[:, cols] = pulled
-        turned = weighted.T
+    def unit_rows(index):
+        chip = jnp.where(index == 0, p, near)
+        mixed = jnp.where(index == 1, hn, 0)
+        return [
+            jnp.where(
+                (index == 0) | (index == 2), chip * 2 * n + i * hn,
+                (jnp.where(i < 2, far, edge) * 2 + i % 2) * n + mixed,
+            ) for i in range(4)
+        ]
+
+    def part_of(i):
+        return pl.ds(pl.multiple_of(i * PART, PART), PART)
+
+    def turn(rows, i, flag):
+        weighted, pulled = weigh(all_ref, wr_ref, rows, hn, part_of(i))
+        gacc_ref[:, part_of(i)] += pulled * flag
+        return weighted
+
+    def multiply(turned, rows, i):
+        value = turned[...]
         for t in range(half // TILE):
             there = pl.ds(t * TILE, TILE)
-            h_ref[cols, there] += jnp.dot(
-                turned, slabs(col_ref, None, first, hn, there),
+            h_ref[part_of(i), there] += jnp.dot(
+                value, slabs(col_ref, None, rows, hn, there),
                 preferred_element_type=jnp.float32,
             )
 
     def compute(u):
-        index = sum((u >= s).astype(jnp.int32) for s in starts) - 1
+        index = sum((u >= s).astype(jnp.int32) for s in begins) - 1
 
         def choose(values):
             out = values[0]
@@ -382,11 +391,10 @@
                 out = jnp.where(index >= i, values[i], out)
             return out
 
-        begin, end = choose(starts), choose(stops)
-        speed = choose([-(-tiles // (e - s)) for s, e in zip(starts, stops)])
-        low = jnp.minimum((u - begin) * speed, tiles)
-        high = jnp.minimum(low + speed, tiles)
-        chip, piece = unit(index)
+        begin, span = choose(begins), choose([e - s for s, e in zip(begins, ends)])
+        low = (u - begin) * tiles // span
+        high = (u - begin + 1) * tiles // span
+        rows = unit_rows(index)
 
         @pl.when(u == begin)
         def _():
@@ -395,20 +403,51 @@
                 own.wait()
                 weights()
                 gacc_ref[...] = jnp.zeros_like(gacc_ref)
-
-            @pl.when((index != 1) & (index != 3))
-            def _():
-                partner_rows(chip)
-
-            @pl.when((index == 5) & (p != z))
+                partner_rows(p)
+
+            @pl.when(index == 1)
+            def _():
+                partner_rows(far)
+                partner_rows(edge)
+
+            @pl.when(index == 2)
+            def _():
+                partner_rows(near)
+
+            @pl.when((index == 3) & (p != z))
             def _():
                 remote(once, once, bf_s.at[0], adr.at[0], rows=r).wait_recv()
 
-        def one(i, _):
-            multiply(chip, piece, i)
+            @pl.when(index != 1)
+            def _():
+                even[...] = turn(rows, 0, 1.0)
+
+        def keep(i, _):
+            for e in range(2):
+                kept[part_of(2 * i + e), :] = turn(rows, 2 * i + e, 1.0)
             return 0
 
-        lax.fori_loop(low, high, one, 0)
+        def pair(i, _):
+            multiply(even, rows, 2 * i)
+            odd[...] = turn(rows, 2 * i + 1, 1.0)
+            multiply(odd, rows, 2 * i + 1)
+            more = i < tiles - 1
+            even[...] = turn(
+                rows, jnp.where(more, 2 * i + 2, 0), jnp.where(more, 1.0, 0.0)
+            )
+            return 0
+
+        @pl.when(index == 1)
+        def _():
+            lax.fori_loop(low, high, keep, 0)
+
+            @pl.when(u == ends[1] - 1)
+            def _():
+                pltpu.make_async_copy(kept, turned_out, lsem.at[3]).start()
+
+        @pl.when(index != 1)
+        def _():
+            lax.fori_loop(low, high, pair, 0)
 
     def step(u, _):
         @pl.when((p != z) & (u < items * nch))
@@ -437,17 +476,17 @@
         def _():
             share_stats()
 
-        @pl.when(u < starts[0])
+        @pl.when(u < begins[0])
         def _():
             def some(i, _):
                 prepare(i)
                 return 0
-            per = -(-tiles // starts[0])
+            per = -(-tiles // begins[0])
             lax.fori_loop(
                 jnp.minimum(u * per, tiles), jnp.minimum(u * per + per, tiles), some, 0
             )
 
-        @pl.when(u >= starts[0])
+        @pl.when((u >= begins[0]) & (u < ends[-1]))
         def _():
             compute(u)
         return 0
@@ -457,6 +496,15 @@
     @pl.when(p != z)
     def _():
         remote(once, once, bf_s.at[0], adr.at[1], rows=r).wait_recv()
+
+    outs = [pltpu.make_async_copy(gacc_ref, pull_out, lsem.at[4])]
+    for i, start in enumerate(unit_rows(1)):
+        outs.append(pltpu.make_async_copy(
+            col_ref.at[pl.ds(pl.multiple_of(start, CHUNK), hn)],
+            cols_out.at[pl.ds(i * hn, hn)], lsem.at[5 + i],
+        ))
+    for copy in outs:
+        copy.start()
 
     def sent(ref, sem):
         remote(ref, ref, sem, pr.at[3], rows=r).wait_send()
@@ -507,6 +555,9 @@
                 @pl.when(more)
                 def _():
                     sent(twice, af_s.at[q])
+    for copy in outs:
+        copy.wait()
+    pltpu.make_async_copy(kept, turned_out, lsem.at[3]).wait()
 
 
 def line_stage(features, stats, prec):
@@ -521,17 +572,24 @@
         functools.partial(line_kernel, row_count, feat_count),
         out_shape=(
             pltpu.VMEM((width, half), jnp.float32),
-            pltpu.VMEM((row_count * n, width), features.dtype),
-            pltpu.VMEM((row_count * n, half), features.dtype),
-            pltpu.VMEM((2, row_count * n, 128), features.dtype),
-            pltpu.VMEM((8, width), jnp.float32),
+            pltpu.HBM((width, 2 * n), features.dtype),
+            pltpu.HBM((2 * n, half), features.dtype),
+            pltpu.HBM((8, width), jnp.float32),
         ),
         in_specs=[
             pl.BlockSpec(memory_space=pl.ANY), pl.BlockSpec(memory_space=pltpu.VMEM),
             pl.BlockSpec(memory_space=pltpu.VMEM),
         ],
-        out_specs=[pl.BlockSpec(memory_space=pltpu.VMEM)] * 5,
+        out_specs=[pl.BlockSpec(memory_space=pltpu.VMEM)]
+        + [pl.BlockSpec(memory_space=pl.ANY)] * 3,
         scratch_shapes=[
+            pltpu.VMEM((row_count * n, width), features.dtype),
+            pltpu.VMEM((row_count * n, half), features.dtype),
+            pltpu.VMEM((2, row_count * n, 128), features.dtype),
+            pltpu.VMEM((8, width), jnp.float32),
+            pltpu.VMEM((width, 2 * n), features.dtype),
+            pltpu.VMEM((PART, 2 * n), features.dtype),
+            pltpu.VMEM((PART, 2 * n), features.dtype),
             pltpu.VMEM((items, 2, n, half), features.dtype),
             pltpu.VMEM((row_count, feat_count) + stats.shape, stats.dtype),
             dma((3, 2, nch)), dma((4,)), dma((items, 2, nch)), dma((items + 1, 2, nch)),
@@ -540,92 +598,105 @@
             dma((items,)), dma((items,)),
             dma((feat_count,)), dma((feat_count,)),
             dma((row_count,)), dma((row_count,)),
-            dma((3,)),
+            dma((9,)),
         ],
         compiler_params=pltpu.CompilerParams(
-            collective_id=0, has_side_effects=True, vmem_limit_bytes=10 * 1024 * 1024
+            collective_id=0, has_side_effects=True, vmem_limit_bytes=30 * 1024 * 1024
         ),
         name="line_stage",
     )(features, stats, prec)
 
 
 def last_kernel(
-    row_count, feat_count, h_ref, all_ref, col_ref, wr_ref, gacc_ref, pull_ref,
-    out_ref, grad_ref, stage, ycols, total, sem,
+    h_ref, turned_ref, cols_ref, gacc_ref, pull_ref,
+    out_ref, grad_ref, stage, turned, cols, gacc, pull, grad, sem, lsem, tsem,
 ):
-    r = lax.axis_index("rows")
-    z = lax.axis_index("feat")
-    p, c = r // 2, r % 2
-    last = feat_count - 1
-    edge = passed_chip(p, z, last)
     width, half = h_ref.shape
-    n = all_ref.shape[0] // row_count
-    hn = n // 2
-    first = [
-        (chip * 2 + k) * n + hn for chip in (edge, pick(p, 2, edge)) for k in range(2)
+    slots = stage.shape[0]
+    count = width // PART
+    load = pltpu.make_async_copy(cols_ref, cols, lsem.at[0])
+    load.start()
+
+    def part_of(i):
+        return pl.ds(pl.multiple_of(i * PART, PART), PART)
+
+    def take(i):
+        return pltpu.make_async_copy(
+            turned_ref.at[part_of(i)], turned.at[part_of(i)], tsem.at[i]
+        )
+
+    def put(i):
+        slot = lax.rem(i, slots)
+        return pltpu.make_async_copy(stage.at[slot], out_ref.at[part_of(i)], sem.at[slot])
+
+    for i in range(count):
+        take(i).start()
+    late = [
+        pltpu.make_async_copy(gacc_ref, gacc, lsem.at[1]),
+        pltpu.make_async_copy(pull_ref, pull, lsem.at[2]),
     ]
-    slots, tile = stage.shape[:2]
-    for i, start in enumerate(first):
-        ycols[pl.ds(i * hn, hn), :] = col_ref[pl.ds(pl.multiple_of(start, CHUNK), hn), :]
-
-    def put(i, slot):
-        rows = pl.ds(pl.multiple_of(i * tile, tile), tile)
-        return pltpu.make_async_copy(stage.at[slot], out_ref.at[rows], sem.at[slot])
+    for copy in late:
+        copy.start()
+    load.wait()
 
     def one(i, _):
+        @pl.when(i >= slots)
+        def _():
+            put(i - slots).wait()
+        take(i).wait()
         slot = lax.rem(i, slots)
-
-        @pl.when(i >= slots)
-        def _():
-            put(i - slots, slot).wait()
-        cols = pl.ds(pl.multiple_of(i * tile, tile), tile)
-        weighted, pulled = weigh(all_ref, wr_ref, gacc_ref, first, hn, cols, tile)
-        grad_ref[:, cols] = jnp.sum(pulled, axis=0, keepdims=True) - pull_ref[:, cols]
-        turned = weighted.T
+        value = turned[part_of(i), :]
         for t in range(half // TILE):
             there = pl.ds(t * TILE, TILE)
-            stage[slot, :, there] = h_ref[cols, there] + jnp.dot(
-                turned, ycols[:, there], preferred_element_type=jnp.float32
+            stage[slot, :, there] = h_ref[part_of(i), there] + jnp.dot(
+                value, cols[:, there], preferred_element_type=jnp.float32
             )
-        put(i, slot).start()
+        put(i).start()
         return 0
 
-    count = width // tile
     lax.fori_loop(0, count, one, 0)
+    for copy in late:
+        copy.wait()
+    grad[...] = jnp.sum(gacc[...], axis=0, keepdims=True) - pull[...]
+    give = pltpu.make_async_copy(grad, grad_ref, lsem.at[3])
+    give.start()
     for i in range(max(0, count - slots), count):
-        put(i, i % slots).wait()
-
-
-def last_stage(h, all_rows, col_rows, wr, gacc, pull):
-    row_count = lax.axis_size("rows")
-    feat_count = lax.axis_size("feat")
+        put(i).wait()
+    give.wait()
+
+
+def last_stage(h, turned, cols, gacc, pull):
     width, half = h.shape
-    n = all_rows.shape[0] // row_count
+    dma = pltpu.SemaphoreType.DMA
+    h = pltpu.with_memory_space_constraint(h, pltpu.VMEM)
+    kept = [pltpu.with_memory_space_constraint(a, pltpu.HBM) for a in (turned, cols, gacc, pull)]
     return pl.pallas_call(
-        functools.partial(last_kernel, row_count, feat_count),
+        last_kernel,
         out_shape=(
-            jax.ShapeDtypeStruct((width, half), jnp.float32),
-            jax.ShapeDtypeStruct((1, width), jnp.float32),
+            pltpu.HBM((width, half), jnp.float32),
+            pltpu.HBM((1, width), jnp.float32),
         ),
-        in_specs=[pl.BlockSpec(memory_space=pltpu.VMEM)] * 6,
-        out_specs=[
-            pl.BlockSpec(memory_space=pl.ANY), pl.BlockSpec(memory_space=pltpu.VMEM),
+        in_specs=[pl.BlockSpec(memory_space=pltpu.VMEM)]
+        + [pl.BlockSpec(memory_space=pl.ANY)] * 4,
+        out_specs=[pl.BlockSpec(memory_space=pl.ANY)] * 2,
+        scratch_shapes=[
+            pltpu.VMEM((3, PART, half), jnp.float32),
+            pltpu.VMEM(turned.shape, turned.dtype),
+            pltpu.VMEM(cols.shape, cols.dtype),
+            pltpu.VMEM(gacc.shape, gacc.dtype),
+            pltpu.VMEM(pull.shape, pull.dtype),
+            pltpu.VMEM(pull.shape, pull.dtype),
+            dma((3,)), dma((4,)), dma((width // PART,)),
         ],
-        scratch_shapes=[
-            pltpu.VMEM((2, 256, half), jnp.float32),
-            pltpu.VMEM((2 * n, half), all_rows.dtype),
-            pltpu.VMEM((8, 128), jnp.float32),
-            pltpu.SemaphoreType.DMA((2,)),
-        ],
-        compiler_params=pltpu.CompilerParams(vmem_limit_bytes=9 * 1024 * 1024),
+        compiler_params=pltpu.CompilerParams(vmem_limit_bytes=14 * 1024 * 1024),
         name="last_stage",
-    )(*[pltpu.with_memory_space_constraint(a, pltpu.VMEM) for a in (h, all_rows, col_rows, wr, gacc)], pull)
+    )(h, *kept)
 
 
 def paired(row_count, feat_count, n, width):
     half = width // 2
     rows = row_count * n
-    held = 4 * width * half + 2 * rows * (width + half) + 12 * n * half
+    held = 4 * width * half + 2 * rows * (width + half + 256) + 12 * n * half + 4 * n * width
     return (
         row_count == 2 * feat_count and (feat_count - 1).bit_length() == 2
         and feat_count & (feat_count - 1) == 0 and n % (6 * CHUNK) == 0

time: 217 us -> 180 us (0.83)
  local copies, waits for them, and re-layouts: 38 us -> 1.33 us
    unnamed x13 -> x1, local copies, waits for them, and re-layouts: 37.4 us -> 0.71 us
    pallas_call x1, Pallas kernels: 18.8 us -> 15.3 us  [last_stage(): pl.pallas_call(last_kernel, out_shape=(pltpu.HBM((width, half), jnp.float...]
    pallas_call x1, Pallas kernels: 155 us -> 158 us  [line_stage(): pl.pallas_call(functools.partial(line_kernel, row_count, feat_count), out...]
where the time goes in v3:
time: 180 us; the launch traced here: 179 us
  Pallas kernels  174 us (97%)
  other arithmetic  2.03 us (1%)
  matrix products  1.92 us (1%)
    pallas_call x1, Pallas kernels, line_stage(): pl.pallas_call(functools.partial(line_kernel, row_count, feat_count), out...  158 us
    pallas_call x1, Pallas kernels, last_stage(): pl.pallas_call(last_kernel, out_shape=(pltpu.HBM((width, half), jnp.float...  15.3 us

profile of v3, /device:TPU:24, one launch (start us, length us, event | category | flops | bytes accessed | tf_op | source)
XLA Modules:
  0.0 179.4 jit_solution(16808130983611796630)
XLA Ops:
  0.6 0.7 convert_element_type.9
  1.3 1.3 convert_multiply_fusion
  2.6 0.7 reshape.20
  3.4 1.9 %fusion = f32[1,192]{1,0:T(1,128)S(1)} fusion(bf16[192,4096]{1,0:T(8,128)(2,1)} %x_ref.1, bf16[4096,1]{0,1:T(2,128)(2,1)S(1)} %reshape.20), kind=kOutput, calls=%fused_computation.2 | convolution fusion | flops 1572864 | bytes 1581824 | tf_op jit(solution)/shard_map/dot_general | solution.py:709
  5.3 0.6 reshape.16.st_ref
  5.9 158.2 %line_stage.1 = (f32[4096,2048]{1,0:T(8,128)S(1)}, bf16[4096,384]{1,0:T(8,128)(2,1)}, bf16[384,2048]{1,0:T(8,128)(2,1)}, f32[8,4096]{1,0:T(8,128)}) custom-call(bf16[192,4096]{1,0:T(8,128)(2,1)} %x_ref.1, f32[16,128]{1,0:T(8,128)} %reshape.16.st_ref, f32[1,4096]{1,0:T(1,128)} %bitcast.8), custom_call_target="tpu_custom_call" | custom-call | tf_op jit(solution)/shard_map/line_stage/pallas_call | solution.py:571
  164.1 15.3 %last_stage.1 = (f32[4096,2048]{1,0:T(8,128)}, f32[1,4096]{1,0:T(1,128)}) custom-call(f32[4096,2048]{1,0:T(8,128)S(1)} %get-tuple-element.8.h_ref, bf16[4096,384]{1,0:T(8,128)(2,1)} %get-tuple-element.9.turned_ref, bf16[384,2048]{1,0:T(8,128)(2,1)} %get-tuple-element.10.cols_ref, f32[8,4096]{1,0:T(8,128)} %get-tuple-element.11.gacc_ref, f32[1,4096]{1,0:T(1,128)} %bitcast.9), custom_call_target="tpu_custom_call" | custom-call | tf_op jit(solution)/shard_map/last_stage/pallas_call | solution.py:673
  (3 shorter events, 0.0 us)

commit v4 on v3

--- a/solution.py
+++ b/solution.py
@@ -12,7 +12,7 @@
 CHUNK = 16
 TILE = 512
 PART = 256
-AHEAD = 3
+AHEAD = 4
 VMEM_BUDGET = 60 * 1024 * 1024
 
 
@@ -251,10 +251,9 @@
             def _():
                 forward(1, 0, j, extra_s.at[1])
 
-        @pl.when(a == 2)
-        def _():
-            arrive(2, 0, j)
-            arrive(2, 1, j)
+    def corner_event(j):
+        arrive(2, 0, j)
+        arrive(2, 1, j)
 
     def source_event(s):
         q, j = 1 + s // nch, s % nch
@@ -308,20 +307,30 @@
                         here, here, af_s.at[q], ar.at[q + 1, k, j],
                         feat=jnp.where(down, z - 1, z + 1),
                     ).start()
+
+    def deliver_event(s):
+        q, j = s // nch, s % nch
+        down = p == 0
+        block = jnp.where(down, z + 1 + q, z - 1 - q)
+        slot = jnp.where(down, block - 1, block)
+
+        @pl.when((block >= 0) & (block <= last))
+        def _():
+            for k in range(2):
                 remote(
-                    here, col_ref.at[rows_of(p, k, j)], ad_s.at[q], adr.at[j // (nch // 2)],
-                    rows=2 * block + c,
+                    abuf.at[slot, k, own_rows(j)], col_ref.at[rows_of(p, k, j)],
+                    ad_s.at[q], adr.at[j // (nch // 2)], rows=2 * block + c,
                 ).start()
 
     items = last
-    lag = nch // 2 + 1
+    lag = nch // 2 + 3
     tiles = width // TILE
     edge = passed_chip(p, z, last)
     twice = col_ref.at[pl.ds(0, 2 * n)]
     once = col_ref.at[pl.ds(0, n)]
     hn = n // 2
     q = nch // 6
-    begins = [6 * q, 10 * q, 12 * q, 15 * q]
+    begins = [6 * q, 11 * q, 12 * q, 15 * q]
     ends = [10 * q, 12 * q, 15 * q, 18 * q]
     near, far = pick(p, 1, edge), pick(p, 2, edge)
 
@@ -392,8 +401,8 @@
             return out
 
         begin, span = choose(begins), choose([e - s for s, e in zip(begins, ends)])
-        low = (u - begin) * tiles // span
-        high = (u - begin + 1) * tiles // span
+        low = jnp.minimum((u - begin) * tiles // span, tiles)
+        high = jnp.minimum((u - begin + 1) * tiles // span, tiles)
         rows = unit_rows(index)
 
         @pl.when(u == begin)
@@ -449,20 +458,33 @@
         def _():
             lax.fori_loop(low, high, pair, 0)
 
+    def some(event, low, high):
+        def one(i, _):
+            event(i)
+            return 0
+        lax.fori_loop(low, high, one, 0)
+
     def step(u, _):
         @pl.when((p != z) & (u < items * nch))
         def _():
             column_event(u)
 
-        @pl.when(u + AHEAD < nch)
-        def _():
-            own_sends(u + AHEAD, 0)
-        for e in range(2):
-            s = 2 * u - 2 + e
-
-            @pl.when((s >= 0) & (s < 3 * nch))
-            def _():
-                gather_event(s)
+        @pl.when(u == 1)
+        def _():
+            share_stats()
+
+        @pl.when((u >= 1) & (4 * (u - 1) + AHEAD < nch))
+        def _():
+            low = 4 * (u - 1) + AHEAD
+            some(lambda j: own_sends(j, 0), low, jnp.minimum(low + 4, nch))
+
+        @pl.when((u >= 3) & (u < 3 + nch))
+        def _():
+            some(gather_event, 2 * u - 6, 2 * u - 4)
+
+        @pl.when((u >= 9 * q) & (u < 11 * q))
+        def _():
+            some(corner_event, 3 * (u - 9 * q), 3 * (u - 9 * q) + 3)
 
         @pl.when((p == z) & (u >= lag) & (u < lag + 2 * nch))
         def _():
@@ -472,19 +494,15 @@
         def _():
             pass_event(u - 1)
 
-        @pl.when(u == 3)
-        def _():
-            share_stats()
+        @pl.when(((p == 0) | (p == last)) & (u >= nch))
+        def _():
+            low = jnp.minimum(2 * (u - nch), u - 1)
+            some(deliver_event, low, jnp.minimum(2 * (u + 1 - nch), u))
 
         @pl.when(u < begins[0])
         def _():
-            def some(i, _):
-                prepare(i)
-                return 0
             per = -(-tiles // begins[0])
-            lax.fori_loop(
-                jnp.minimum(u * per, tiles), jnp.minimum(u * per + per, tiles), some, 0
-            )
+            some(prepare, jnp.minimum(u * per, tiles), jnp.minimum(u * per + per, tiles))
 
         @pl.when((u >= begins[0]) & (u < ends[-1]))
         def _():

time: 180 us -> 145 us (0.81)
  Pallas kernels: 174 us -> 137 us
    pallas_call x1, Pallas kernels: 158 us -> 122 us  [line_stage(): pl.pallas_call(functools.partial(line_kernel, row_count, feat_count), out...]
where the time goes in v4:
time: 145 us; the launch traced here: 143 us
  Pallas kernels  137 us (94%)
  other arithmetic  2.03 us (1%)
  matrix products  1.92 us (1%)
    pallas_call x1, Pallas kernels, line_stage(): pl.pallas_call(functools.partial(line_kernel, row_count, feat_count), out...  122 us
    pallas_call x1, Pallas kernels, last_stage(): pl.pallas_call(last_kernel, out_shape=(pltpu.HBM((width, half), jnp.float...  15.3 us

profile of v4, /device:TPU:24, one launch (start us, length us, event | category | flops | bytes accessed | tf_op | source)
XLA Modules:
  0.0 143.0 jit_solution(7490932772807843976)
XLA Ops:
  0.6 0.7 convert_element_type.9
  1.3 1.3 convert_multiply_fusion
  2.6 0.7 reshape.20
  3.4 1.9 %fusion = f32[1,192]{1,0:T(1,128)S(1)} fusion(bf16[192,4096]{1,0:T(8,128)(2,1)} %x_ref.1, bf16[4096,1]{0,1:T(2,128)(2,1)S(1)} %reshape.20), kind=kOutput, calls=%fused_computation.2 | convolution fusion | flops 1572864 | bytes 1581824 | tf_op jit(solution)/shard_map/dot_general | solution.py:727
  5.3 0.6 reshape.16.st_ref
  5.9 121.8 %line_stage.1 = (f32[4096,2048]{1,0:T(8,128)S(1)}, bf16[4096,384]{1,0:T(8,128)(2,1)}, bf16[384,2048]{1,0:T(8,128)(2,1)}, f32[8,4096]{1,0:T(8,128)}) custom-call(bf16[192,4096]{1,0:T(8,128)(2,1)} %x_ref.1, f32[16,128]{1,0:T(8,128)} %reshape.16.st_ref, f32[1,4096]{1,0:T(1,128)} %bitcast.8), custom_call_target="tpu_custom_call" | custom-call | tf_op jit(solution)/shard_map/line_stage/pallas_call | solution.py:589
  127.8 15.3 %last_stage.1 = (f32[4096,2048]{1,0:T(8,128)}, f32[1,4096]{1,0:T(1,128)}) custom-call(f32[4096,2048]{1,0:T(8,128)S(1)} %get-tuple-element.8.h_ref, bf16[4096,384]{1,0:T(8,128)(2,1)} %get-tuple-element.9.turned_ref, bf16[384,2048]{1,0:T(8,128)(2,1)} %get-tuple-element.10.cols_ref, f32[8,4096]{1,0:T(8,128)} %get-tuple-element.11.gacc_ref, f32[1,4096]{1,0:T(1,128)} %bitcast.9), custom_call_target="tpu_custom_call" | custom-call | tf_op jit(solution)/shard_map/last_stage/pallas_call | solution.py:691
  (3 shorter events, 0.0 us)

commit v5 on v4

--- a/solution.py
+++ b/solution.py
@@ -12,7 +12,7 @@
 CHUNK = 16
 TILE = 512
 PART = 256
-AHEAD = 4
+AHEAD = 2
 VMEM_BUDGET = 60 * 1024 * 1024
 
 
@@ -48,9 +48,9 @@
 
 
 def line_kernel(
-    row_count, feat_count, x_ref, st_ref, prec_ref,
+    row_count, feat_count, x_ref, label_ref, post_ref, prec_ref,
     h_ref, turned_out, cols_out, pull_out,
-    all_ref, col_ref, wr_ref, gacc_ref, kept, even, odd, abuf, stat_ref,
+    all_ref, col_ref, wr_ref, gacc_ref, kept, even, odd, abuf, st_ref, stat_ref,
     agr, pr, br, ar, adr, own_s, relay_s, extra_s, part_s, src_s, bf_s, af_s, ad_s,
     ss, sr, ts, tr, lsem,
 ):
@@ -97,6 +97,92 @@
             )
     pl.semaphore_wait(barrier, row_count - 1 + 2 * (feat_count - 1))
 
+    def ag(dim, h, j, src, chip, rel, send):
+        remote(
+            src, all_ref.at[rows_of(chip, c, j), cols_of(h)],
+            send, agr.at[rel, h, j], rows=r ^ (2 * dim),
+        ).start()
+
+    def own_plane(s):
+        j = lax.rem(s, nch)
+
+        @pl.when(s < nch)
+        def _():
+            ag(1, 0, j, x_ref.at[own_rows(j), cols_of(0)], p, 0, own_s.at[0])
+            ag(2, 1, j, x_ref.at[own_rows(j), cols_of(1)], p, 1, own_s.at[1])
+
+        @pl.when(s >= nch)
+        def _():
+            ag(1, 1, j, x_ref.at[own_rows(j), cols_of(1)], p, 0, own_s.at[0])
+            ag(2, 0, j, x_ref.at[own_rows(j), cols_of(0)], p, 1, own_s.at[1])
+
+    def own_line(j):
+        for h in range(2):
+            src = x_ref.at[own_rows(j), cols_of(h)]
+
+            @pl.when(has_down & (p == 0))
+            def _():
+                remote(
+                    src, abuf.at[z - 1, c, own_rows(j)], own_s.at[2], ar.at[0, c, j],
+                    rows=2 * p + h, feat=z - 1,
+                ).start()
+
+            @pl.when(has_down & (p == z))
+            def _():
+                remote(
+                    src, col_ref.at[rows_of(p, c, j)], own_s.at[2], br.at[0, c, j],
+                    rows=2 * p + h, feat=z - 1,
+                ).start()
+
+            @pl.when(has_up & (p == last))
+            def _():
+                remote(
+                    src, abuf.at[z, c, own_rows(j)], own_s.at[3], ar.at[0, c, j],
+                    rows=2 * p + h, feat=z + 1,
+                ).start()
+
+            @pl.when(has_up & (p == z))
+            def _():
+                remote(
+                    src, col_ref.at[rows_of(p, c, j)], own_s.at[3], br.at[0, c, j],
+                    rows=2 * p + h, feat=z + 1,
+                ).start()
+
+    def own_sends(j, _):
+        own_plane(2 * j)
+        own_plane(2 * j + 1)
+        own_line(j)
+        return 0
+
+    own = pltpu.make_async_copy(
+        x_ref, all_ref.at[pl.ds(pl.multiple_of(r * n, n), n)], lsem.at[1]
+    )
+    own.start()
+    lax.fori_loop(0, AHEAD, own_sends, 0)
+    remote(
+        x_ref, all_ref.at[pl.ds(pl.multiple_of(r * n, n), n)], part_s.at[3], pr.at[3],
+        rows=r ^ 1,
+    ).start()
+
+    own.wait()
+    st_ref[...] = jnp.zeros_like(st_ref)
+    post = post_ref[...].astype(jnp.float32)
+    for t in range(-(-n // 128)):
+        count = min(128, n - 128 * t)
+        here = pl.ds(128 * t, count)
+        st_ref[8 + t:9 + t, 0:count] = label_ref[:, here].astype(jnp.float32)
+        rows = pl.ds(pl.multiple_of(r * n + 128 * t, CHUNK), count)
+
+        total = jnp.zeros((count, 128), jnp.float32)
+        for i in range(width // 128):
+            value = all_ref[rows, pl.ds(128 * i, 128)].astype(jnp.float32)
+            total = total + value * post[i:i + 1, :]
+        st_ref[t:t + 1, 0:count] = jnp.sum(total.T, axis=0, keepdims=True)
+    gacc_ref[...] = jnp.zeros_like(gacc_ref)
+    for t in range(width // 128):
+        lanes = pl.ds(128 * t, 128)
+        gacc_ref[0:1, lanes] = -prec_ref[:, lanes] * post[t:t + 1, :]
+    lax.fori_loop(AHEAD, 2 * AHEAD, own_sends, 0)
     stat_local = pltpu.make_async_copy(st_ref, stat_ref.at[r, z], lsem.at[0])
     stat_local.start()
     for d in range(1, feat_count):
@@ -104,73 +190,6 @@
             st_ref, stat_ref.at[r, z], ss.at[d], sr.at[d],
             feat=lax.rem(z + d, feat_count),
         ).start()
-
-    def ag(dim, h, j, src, chip, rel, send):
-        remote(
-            src, all_ref.at[rows_of(chip, c, j), cols_of(h)],
-            send, agr.at[rel, h, j], rows=r ^ (2 * dim),
-        ).start()
-
-    def own_plane(s):
-        j = lax.rem(s, nch)
-
-        @pl.when(s < nch)
-        def _():
-            ag(1, 0, j, x_ref.at[own_rows(j), cols_of(0)], p, 0, own_s.at[0])
-            ag(2, 1, j, x_ref.at[own_rows(j), cols_of(1)], p, 1, own_s.at[1])
-
-        @pl.when(s >= nch)
-        def _():
-            ag(1, 1, j, x_ref.at[own_rows(j), cols_of(1)], p, 0, own_s.at[0])
-            ag(2, 0, j, x_ref.at[own_rows(j), cols_of(0)], p, 1, own_s.at[1])
-
-    def own_line(j):
-        for h in range(2):
-            src = x_ref.at[own_rows(j), cols_of(h)]
-
-            @pl.when(has_down & (p == 0))
-            def _():
-                remote(
-                    src, abuf.at[z - 1, c, own_rows(j)], own_s.at[2], ar.at[0, c, j],
-                    rows=2 * p + h, feat=z - 1,
-                ).start()
-
-            @pl.when(has_down & (p == z))
-            def _():
-                remote(
-                    src, col_ref.at[rows_of(p, c, j)], own_s.at[2], br.at[0, c, j],
-                    rows=2 * p + h, feat=z - 1,
-                ).start()
-
-            @pl.when(has_up & (p == last))
-            def _():
-                remote(
-                    src, abuf.at[z, c, own_rows(j)], own_s.at[3], ar.at[0, c, j],
-                    rows=2 * p + h, feat=z + 1,
-                ).start()
-
-            @pl.when(has_up & (p == z))
-            def _():
-                remote(
-                    src, col_ref.at[rows_of(p, c, j)], own_s.at[3], br.at[0, c, j],
-                    rows=2 * p + h, feat=z + 1,
-                ).start()
-
-    def own_sends(j, _):
-        own_plane(2 * j)
-        own_plane(2 * j + 1)
-        own_line(j)
-        return 0
-
-    own = pltpu.make_async_copy(
-        x_ref, all_ref.at[pl.ds(pl.multiple_of(r * n, n), n)], lsem.at[1]
-    )
-    lax.fori_loop(0, AHEAD, own_sends, 0)
-    own.start()
-    remote(
-        x_ref, all_ref.at[pl.ds(pl.multiple_of(r * n, n), n)], part_s.at[3], pr.at[3],
-        rows=r ^ 1,
-    ).start()
 
     def share_stats():
         stat_local.wait()
@@ -319,7 +338,7 @@
             for k in range(2):
                 remote(
                     abuf.at[slot, k, own_rows(j)], col_ref.at[rows_of(p, k, j)],
-                    ad_s.at[q], adr.at[j // (nch // 2)], rows=2 * block + c,
+                    ad_s.at[q], adr.at[j // (nch // 3)], rows=2 * block + c,
                 ).start()
 
     items = last
@@ -327,11 +346,11 @@
     tiles = width // TILE
     edge = passed_chip(p, z, last)
     twice = col_ref.at[pl.ds(0, 2 * n)]
-    once = col_ref.at[pl.ds(0, n)]
-    hn = n // 2
-    q = nch // 6
-    begins = [6 * q, 11 * q, 12 * q, 15 * q]
-    ends = [10 * q, 12 * q, 15 * q, 18 * q]
+    third = n // 3
+    once = col_ref.at[pl.ds(0, 2 * third)]
+    q = nch // 3
+    begins = [3 * q, 4 * q + 1, 5 * q + 1, 6 * q, 7 * q, 8 * q]
+    ends = [4 * q, 5 * q + 1, 6 * q, 7 * q, 8 * q, 9 * q]
     near, far = pick(p, 1, edge), pick(p, 2, edge)
 
     def partner_rows(chip):
@@ -365,20 +384,29 @@
             )
 
     def unit_rows(index):
-        chip = jnp.where(index == 0, p, near)
-        mixed = jnp.where(index == 1, hn, 0)
-        return [
-            jnp.where(
-                (index == 0) | (index == 2), chip * 2 * n + i * hn,
-                (jnp.where(i < 2, far, edge) * 2 + i % 2) * n + mixed,
-            ) for i in range(4)
-        ]
+        def start(chip, core, piece):
+            return (chip * 2 + core) * n + piece * third
+
+        late = jnp.where(index == 2, 2, index - 4 + (index == 3))
+        rows = []
+        for i in range(4):
+            core, upper = i % 2, i // 2
+            pair = jnp.where(
+                index == 0, start(p, core, upper),
+                jnp.where(
+                    index == 1, start(near if upper else p, core, 0 if upper else 2),
+                    start(near, core, 1 + upper),
+                ),
+            )
+            far_rows = start(edge if upper else far, core, late)
+            rows.append(jnp.where((index == 0) | (index == 1) | (index == 3), pair, far_rows))
+        return rows
 
     def part_of(i):
         return pl.ds(pl.multiple_of(i * PART, PART), PART)
 
     def turn(rows, i, flag):
-        weighted, pulled = weigh(all_ref, wr_ref, rows, hn, part_of(i))
+        weighted, pulled = weigh(all_ref, wr_ref, rows, third, part_of(i))
         gacc_ref[:, part_of(i)] += pulled * flag
         return weighted
 
@@ -387,7 +415,7 @@
         for t in range(half // TILE):
             there = pl.ds(t * TILE, TILE)
             h_ref[part_of(i), there] += jnp.dot(
-                value, slabs(col_ref, None, rows, hn, there),
+                value, slabs(col_ref, None, rows, third, there),
                 preferred_element_type=jnp.float32,
             )
 
@@ -409,25 +437,23 @@
         def _():
             @pl.when(index == 0)
             def _():
-                own.wait()
                 weights()
-                gacc_ref[...] = jnp.zeros_like(gacc_ref)
                 partner_rows(p)
 
             @pl.when(index == 1)
+            def _():
+                partner_rows(near)
+
+            @pl.when(index == 2)
             def _():
                 partner_rows(far)
                 partner_rows(edge)
 
-            @pl.when(index == 2)
-            def _():
-                partner_rows(near)
-
-            @pl.when((index == 3) & (p != z))
-            def _():
-                remote(once, once, bf_s.at[0], adr.at[0], rows=r).wait_recv()
-
-            @pl.when(index != 1)
+            @pl.when((index >= 4) & (p != z))
+            def _():
+                remote(once, once, bf_s.at[0], adr.at[index - 4], rows=r).wait_recv()
+
+            @pl.when(index != 2)
             def _():
                 even[...] = turn(rows, 0, 1.0)
 
@@ -446,15 +472,15 @@
             )
             return 0
 
-        @pl.when(index == 1)
+        @pl.when(index == 2)
         def _():
             lax.fori_loop(low, high, keep, 0)
 
-            @pl.when(u == ends[1] - 1)
+            @pl.when(u == ends[2] - 1)
             def _():
                 pltpu.make_async_copy(kept, turned_out, lsem.at[3]).start()
 
-        @pl.when(index != 1)
+        @pl.when(index != 2)
         def _():
             lax.fori_loop(low, high, pair, 0)
 
@@ -469,22 +495,28 @@
         def _():
             column_event(u)
 
-        @pl.when(u == 1)
+        @pl.when(u == 3)
         def _():
             share_stats()
 
-        @pl.when((u >= 1) & (4 * (u - 1) + AHEAD < nch))
-        def _():
-            low = 4 * (u - 1) + AHEAD
-            some(lambda j: own_sends(j, 0), low, jnp.minimum(low + 4, nch))
+        @pl.when((u >= 1) & (u < 3))
+        def _():
+            own_sends(2 * AHEAD - 1 + u, 0)
+
+        @pl.when(u >= 3)
+        def _():
+            low = 2 * AHEAD + 2 + 2 * (u - 3)
+            some(lambda j: own_sends(j, 0), low, jnp.minimum(low + 2, nch))
 
         @pl.when((u >= 3) & (u < 3 + nch))
         def _():
             some(gather_event, 2 * u - 6, 2 * u - 4)
 
-        @pl.when((u >= 9 * q) & (u < 11 * q))
-        def _():
-            some(corner_event, 3 * (u - 9 * q), 3 * (u - 9 * q) + 3)
+        corner = 9 * q // 2
+
+        @pl.when((u >= corner) & (u < corner + q))
+        def _():
+            some(corner_event, 3 * (u - corner), 3 * (u - corner) + 3)
 
         @pl.when((p == z) & (u >= lag) & (u < lag + 2 * nch))
         def _():
@@ -513,13 +545,13 @@
 
     @pl.when(p != z)
     def _():
-        remote(once, once, bf_s.at[0], adr.at[1], rows=r).wait_recv()
+        remote(once, once, bf_s.at[0], adr.at[2], rows=r).wait_recv()
 
     outs = [pltpu.make_async_copy(gacc_ref, pull_out, lsem.at[4])]
-    for i, start in enumerate(unit_rows(1)):
+    for i, start in enumerate(unit_rows(jnp.int32(2))):
         outs.append(pltpu.make_async_copy(
-            col_ref.at[pl.ds(pl.multiple_of(start, CHUNK), hn)],
-            cols_out.at[pl.ds(i * hn, hn)], lsem.at[5 + i],
+            col_ref.at[pl.ds(pl.multiple_of(start, CHUNK), third)],
+            cols_out.at[pl.ds(i * third, third)], lsem.at[5 + i],
         ))
     for copy in outs:
         copy.start()
@@ -578,7 +610,7 @@
     pltpu.make_async_copy(kept, turned_out, lsem.at[3]).wait()
 
 
-def line_stage(features, stats, prec):
+def line_stage(features, labels, post, prec):
     row_count = lax.axis_size("rows")
     feat_count = lax.axis_size("feat")
     n, width = features.shape
@@ -590,13 +622,13 @@
         functools.partial(line_kernel, row_count, feat_count),
         out_shape=(
             pltpu.VMEM((width, half), jnp.float32),
-            pltpu.HBM((width, 2 * n), features.dtype),
-            pltpu.HBM((2 * n, half), features.dtype),
+            pltpu.HBM((width, 4 * n // 3), features.dtype),
+            pltpu.HBM((4 * n // 3, half), features.dtype),
             pltpu.HBM((8, width), jnp.float32),
         ),
         in_specs=[
             pl.BlockSpec(memory_space=pl.ANY), pl.BlockSpec(memory_space=pltpu.VMEM),
-            pl.BlockSpec(memory_space=pltpu.VMEM),
+            pl.BlockSpec(memory_space=pltpu.VMEM), pl.BlockSpec(memory_space=pltpu.VMEM),
         ],
         out_specs=[pl.BlockSpec(memory_space=pltpu.VMEM)]
         + [pl.BlockSpec(memory_space=pl.ANY)] * 3,
@@ -605,13 +637,14 @@
             pltpu.VMEM((row_count * n, half), features.dtype),
             pltpu.VMEM((2, row_count * n, 128), features.dtype),
             pltpu.VMEM((8, width), jnp.float32),
-            pltpu.VMEM((width, 2 * n), features.dtype),
-            pltpu.VMEM((PART, 2 * n), features.dtype),
-            pltpu.VMEM((PART, 2 * n), features.dtype),
+            pltpu.VMEM((width, 4 * n // 3), features.dtype),
+            pltpu.VMEM((PART, 4 * n // 3), features.dtype),
+            pltpu.VMEM((PART, 4 * n // 3), features.dtype),
             pltpu.VMEM((items, 2, n, half), features.dtype),
-            pltpu.VMEM((row_count, feat_count) + stats.shape, stats.dtype),
+            pltpu.VMEM((16, 128), jnp.float32),
+            pltpu.VMEM((row_count, feat_count, 16, 128), jnp.float32),
             dma((3, 2, nch)), dma((4,)), dma((items, 2, nch)), dma((items + 1, 2, nch)),
-            dma((2,)),
+            dma((3,)),
             dma((4,)), dma((2,)), dma((2,)), dma((4,)), dma((2, items)), dma((items,)),
             dma((items,)), dma((items,)),
             dma((feat_count,)), dma((feat_count,)),
@@ -622,12 +655,12 @@
             collective_id=0, has_side_effects=True, vmem_limit_bytes=30 * 1024 * 1024
         ),
         name="line_stage",
-    )(features, stats, prec)
+    )(features, labels, post, prec)
 
 
 def last_kernel(
-    h_ref, turned_ref, cols_ref, gacc_ref, pull_ref,
-    out_ref, grad_ref, stage, turned, cols, gacc, pull, grad, sem, lsem, tsem,
+    h_ref, turned_ref, cols_ref, gacc_ref,
+    out_ref, grad_ref, stage, turned, cols, gacc, grad, sem, lsem, tsem,
 ):
     width, half = h_ref.shape
     slots = stage.shape[0]
@@ -649,12 +682,8 @@
 
     for i in range(count):
         take(i).start()
-    late = [
-        pltpu.make_async_copy(gacc_ref, gacc, lsem.at[1]),
-        pltpu.make_async_copy(pull_ref, pull, lsem.at[2]),
-    ]
-    for copy in late:
-        copy.start()
+    late = pltpu.make_async_copy(gacc_ref, gacc, lsem.at[1])
+    late.start()
     load.wait()
 
     def one(i, _):
@@ -673,21 +702,20 @@
         return 0
 
     lax.fori_loop(0, count, one, 0)
-    for copy in late:
-        copy.wait()
-    grad[...] = jnp.sum(gacc[...], axis=0, keepdims=True) - pull[...]
-    give = pltpu.make_async_copy(grad, grad_ref, lsem.at[3])
+    late.wait()
+    grad[...] = jnp.sum(gacc[...], axis=0, keepdims=True)
+    give = pltpu.make_async_copy(grad, grad_ref, lsem.at[2])
     give.start()
     for i in range(max(0, count - slots), count):
         put(i).wait()
     give.wait()
 
 
-def last_stage(h, turned, cols, gacc, pull):
+def last_stage(h, turned, cols, gacc):
     width, half = h.shape
     dma = pltpu.SemaphoreType.DMA
     h = pltpu.with_memory_space_constraint(h, pltpu.VMEM)
-    kept = [pltpu.with_memory_space_constraint(a, pltpu.HBM) for a in (turned, cols, gacc, pull)]
+    kept = [pltpu.with_memory_space_constraint(a, pltpu.HBM) for a in (turned, cols, gacc)]
     return pl.pallas_call(
         last_kernel,
         out_shape=(
@@ -695,16 +723,15 @@
             pltpu.HBM((1, width), jnp.float32),
         ),
         in_specs=[pl.BlockSpec(memory_space=pltpu.VMEM)]
-        + [pl.BlockSpec(memory_space=pl.ANY)] * 4,
+        + [pl.BlockSpec(memory_space=pl.ANY)] * 3,
         out_specs=[pl.BlockSpec(memory_space=pl.ANY)] * 2,
         scratch_shapes=[
             pltpu.VMEM((3, PART, half), jnp.float32),
             pltpu.VMEM(turned.shape, turned.dtype),
             pltpu.VMEM(cols.shape, cols.dtype),
             pltpu.VMEM(gacc.shape, gacc.dtype),
-            pltpu.VMEM(pull.shape, pull.dtype),
-            pltpu.VMEM(pull.shape, pull.dtype),
-            dma((3,)), dma((4,)), dma((width // PART,)),
+            pltpu.VMEM((1, width), jnp.float32),
+            dma((3,)), dma((3,)), dma((width // PART,)),
         ],
         compiler_params=pltpu.CompilerParams(vmem_limit_bytes=14 * 1024 * 1024),
         name="last_stage",
@@ -717,21 +744,18 @@
     held = 4 * width * half + 2 * rows * (width + half + 256) + 12 * n * half + 4 * n * width
     return (
         row_count == 2 * feat_count and (feat_count - 1).bit_length() == 2
-        and feat_count & (feat_count - 1) == 0 and n % (6 * CHUNK) == 0
+        and feat_count & (feat_count - 1) == 0 and n % (3 * CHUNK) == 0 and n // CHUNK >= 3 * AHEAD + 3
         and n <= 1024 and half % TILE == 0 and held <= VMEM_BUDGET
     )
 
 
 def by_lines(features, labels, posterior, prior_prec):
     n, width = features.shape
-    partial_value = jnp.dot(features, posterior, preferred_element_type=jnp.float32)
-    stats = jnp.stack([
-        jnp.pad(partial_value, (0, 1024 - n)),
-        jnp.pad(labels.astype(jnp.float32), (0, 1024 - n)),
-    ]).reshape(-1, 128)
-    pull = (prior_prec * posterior.astype(jnp.float32)).reshape(1, width)
-    held = line_stage(features, stats, prior_prec.reshape(1, width))
-    hessian, gradient = last_stage(*held, pull)
+    held = line_stage(
+        features, labels.reshape(1, n), posterior.reshape(width // 128, 128),
+        prior_prec.reshape(1, width),
+    )
+    hessian, gradient = last_stage(*held)
     return (hessian, gradient.reshape(width))
 
 

time: 145 us -> 146 us (level)
  Pallas kernels: 137 us -> 143 us
  other arithmetic: 2.03 us -> 0 us
  matrix products: 1.92 us -> 0 us
    pallas_call x1, Pallas kernels: 122 us -> 130 us  [line_stage(): pl.pallas_call(functools.partial(line_kernel, row_count, feat_count), out...]
    dot_general x1 -> x0, matrix products: 1.92 us -> none  [by_lines(): jnp.dot(features, posterior, preferred_element_type=jnp.float32)]
    pallas_call x1, Pallas kernels: 15.3 us -> 13.4 us  [last_stage(): pl.pallas_call(last_kernel, out_shape=(pltpu.HBM((width, half), jnp.float...]
where the time goes in v5:
time: 146 us; the launch traced here: 144 us
  Pallas kernels  143 us (98%)
    pallas_call x1, Pallas kernels, line_stage(): pl.pallas_call(functools.partial(line_kernel, row_count, feat_count), out...  130 us
    pallas_call x1, Pallas kernels, last_stage(): pl.pallas_call(last_kernel, out_shape=(pltpu.HBM((width, half), jnp.float...  13.4 us

profile of v5, /device:TPU:24, one launch (start us, length us, event | category | flops | bytes accessed | tf_op | source)
XLA Modules:
  0.0 144.1 jit_solution(7162055619716355077)
XLA Ops:
  0.6 130.1 %line_stage.1 = (f32[4096,2048]{1,0:T(8,128)S(1)}, bf16[4096,256]{1,0:T(8,128)(2,1)}, bf16[256,2048]{1,0:T(8,128)(2,1)}, f32[8,4096]{1,0:T(8,128)}) custom-call(bf16[192,4096]{1,0:T(8,128)(2,1)} %x_ref.1, s32[1,192]{1,0:T(1,128)} %bitcast.6, bf16[32,128]{1,0:T(8,128)(2,1)} %bitcast.5, f32[1,4096]{1,0:T(1,128)} %bitcast.4), custom_call_target="tpu_custom_call" | custom-call | tf_op jit(solution)/shard_map/line_stage/pallas_call | solution.py:621
  130.7 13.4 %last_stage.1 = (f32[4096,2048]{1,0:T(8,128)}, f32[1,4096]{1,0:T(1,128)}) custom-call(f32[4096,2048]{1,0:T(8,128)S(1)} %get-tuple-element.8.h_ref, bf16[4096,256]{1,0:T(8,128)(2,1)} %get-tuple-element.9.turned_ref, bf16[256,2048]{1,0:T(8,128)(2,1)} %get-tuple-element.10.cols_ref, f32[8,4096]{1,0:T(8,128)} %get-tuple-element.11.gacc_ref), custom_call_target="tpu_custom_call" | custom-call | tf_op jit(solution)/shard_map/last_stage/pallas_call | solution.py:719

commit v6 on v5

--- a/solution.py
+++ b/solution.py
@@ -13,6 +13,7 @@
 TILE = 512
 PART = 256
 AHEAD = 2
+LATE = 4
 VMEM_BUDGET = 60 * 1024 * 1024
 
 
@@ -95,75 +96,11 @@
                 device_id={"rows": other, "feat": lax.rem(z + d, feat_count)},
                 device_id_type=MESH,
             )
-    pl.semaphore_wait(barrier, row_count - 1 + 2 * (feat_count - 1))
-
-    def ag(dim, h, j, src, chip, rel, send):
-        remote(
-            src, all_ref.at[rows_of(chip, c, j), cols_of(h)],
-            send, agr.at[rel, h, j], rows=r ^ (2 * dim),
-        ).start()
-
-    def own_plane(s):
-        j = lax.rem(s, nch)
-
-        @pl.when(s < nch)
-        def _():
-            ag(1, 0, j, x_ref.at[own_rows(j), cols_of(0)], p, 0, own_s.at[0])
-            ag(2, 1, j, x_ref.at[own_rows(j), cols_of(1)], p, 1, own_s.at[1])
-
-        @pl.when(s >= nch)
-        def _():
-            ag(1, 1, j, x_ref.at[own_rows(j), cols_of(1)], p, 0, own_s.at[0])
-            ag(2, 0, j, x_ref.at[own_rows(j), cols_of(0)], p, 1, own_s.at[1])
-
-    def own_line(j):
-        for h in range(2):
-            src = x_ref.at[own_rows(j), cols_of(h)]
-
-            @pl.when(has_down & (p == 0))
-            def _():
-                remote(
-                    src, abuf.at[z - 1, c, own_rows(j)], own_s.at[2], ar.at[0, c, j],
-                    rows=2 * p + h, feat=z - 1,
-                ).start()
-
-            @pl.when(has_down & (p == z))
-            def _():
-                remote(
-                    src, col_ref.at[rows_of(p, c, j)], own_s.at[2], br.at[0, c, j],
-                    rows=2 * p + h, feat=z - 1,
-                ).start()
-
-            @pl.when(has_up & (p == last))
-            def _():
-                remote(
-                    src, abuf.at[z, c, own_rows(j)], own_s.at[3], ar.at[0, c, j],
-                    rows=2 * p + h, feat=z + 1,
-                ).start()
-
-            @pl.when(has_up & (p == z))
-            def _():
-                remote(
-                    src, col_ref.at[rows_of(p, c, j)], own_s.at[3], br.at[0, c, j],
-                    rows=2 * p + h, feat=z + 1,
-                ).start()
-
-    def own_sends(j, _):
-        own_plane(2 * j)
-        own_plane(2 * j + 1)
-        own_line(j)
-        return 0
 
     own = pltpu.make_async_copy(
         x_ref, all_ref.at[pl.ds(pl.multiple_of(r * n, n), n)], lsem.at[1]
     )
     own.start()
-    lax.fori_loop(0, AHEAD, own_sends, 0)
-    remote(
-        x_ref, all_ref.at[pl.ds(pl.multiple_of(r * n, n), n)], part_s.at[3], pr.at[3],
-        rows=r ^ 1,
-    ).start()
-
     own.wait()
     st_ref[...] = jnp.zeros_like(st_ref)
     post = post_ref[...].astype(jnp.float32)
@@ -182,7 +119,71 @@
     for t in range(width // 128):
         lanes = pl.ds(128 * t, 128)
         gacc_ref[0:1, lanes] = -prec_ref[:, lanes] * post[t:t + 1, :]
-    lax.fori_loop(AHEAD, 2 * AHEAD, own_sends, 0)
+    pl.semaphore_wait(barrier, row_count - 1 + 2 * (feat_count - 1))
+
+    def ag(dim, h, j, src, chip, rel, send):
+        remote(
+            src, all_ref.at[rows_of(chip, c, j), cols_of(h)],
+            send, agr.at[rel, h, j], rows=r ^ (2 * dim),
+        ).start()
+
+    def own_plane(s):
+        j = lax.rem(s, nch)
+
+        @pl.when(s < nch)
+        def _():
+            ag(1, 0, j, x_ref.at[own_rows(j), cols_of(0)], p, 0, own_s.at[0])
+            ag(2, 1, j, x_ref.at[own_rows(j), cols_of(1)], p, 1, own_s.at[1])
+
+        @pl.when(s >= nch)
+        def _():
+            ag(1, 1, j, x_ref.at[own_rows(j), cols_of(1)], p, 0, own_s.at[0])
+            ag(2, 0, j, x_ref.at[own_rows(j), cols_of(0)], p, 1, own_s.at[1])
+
+    def own_line(j):
+        for h in range(2):
+            src = x_ref.at[own_rows(j), cols_of(h)]
+
+            @pl.when(has_down & (p == 0))
+            def _():
+                remote(
+                    src, abuf.at[z - 1, c, own_rows(j)], own_s.at[2], ar.at[0, c, j],
+                    rows=2 * p + h, feat=z - 1,
+                ).start()
+
+            @pl.when(has_down & (p == z))
+            def _():
+                remote(
+                    src, col_ref.at[rows_of(p, c, j)], own_s.at[2], br.at[0, c, j],
+                    rows=2 * p + h, feat=z - 1,
+                ).start()
+
+            @pl.when(has_up & (p == last))
+            def _():
+                remote(
+                    src, abuf.at[z, c, own_rows(j)], own_s.at[3], ar.at[0, c, j],
+                    rows=2 * p + h, feat=z + 1,
+                ).start()
+
+            @pl.when(has_up & (p == z))
+            def _():
+                remote(
+                    src, col_ref.at[rows_of(p, c, j)], own_s.at[3], br.at[0, c, j],
+                    rows=2 * p + h, feat=z + 1,
+                ).start()
+
+    def own_sends(j, _):
+        own_plane(2 * j)
+        own_plane(2 * j + 1)
+        own_line(j)
+        return 0
+
+    own_sends(0, 0)
+    remote(
+        x_ref, all_ref.at[pl.ds(pl.multiple_of(r * n, n), n)], part_s.at[3], pr.at[3],
+        rows=r ^ 1,
+    ).start()
+
     stat_local = pltpu.make_async_copy(st_ref, stat_ref.at[r, z], lsem.at[0])
     stat_local.start()
     for d in range(1, feat_count):
@@ -491,46 +492,6 @@
         lax.fori_loop(low, high, one, 0)
 
     def step(u, _):
-        @pl.when((p != z) & (u < items * nch))
-        def _():
-            column_event(u)
-
-        @pl.when(u == 3)
-        def _():
-            share_stats()
-
-        @pl.when((u >= 1) & (u < 3))
-        def _():
-            own_sends(2 * AHEAD - 1 + u, 0)
-
-        @pl.when(u >= 3)
-        def _():
-            low = 2 * AHEAD + 2 + 2 * (u - 3)
-            some(lambda j: own_sends(j, 0), low, jnp.minimum(low + 2, nch))
-
-        @pl.when((u >= 3) & (u < 3 + nch))
-        def _():
-            some(gather_event, 2 * u - 6, 2 * u - 4)
-
-        corner = 9 * q // 2
-
-        @pl.when((u >= corner) & (u < corner + q))
-        def _():
-            some(corner_event, 3 * (u - corner), 3 * (u - corner) + 3)
-
-        @pl.when((p == z) & (u >= lag) & (u < lag + 2 * nch))
-        def _():
-            source_event(u - lag)
-
-        @pl.when(((p == 0) | (p == last)) & (u >= 1) & (u < 1 + items * nch))
-        def _():
-            pass_event(u - 1)
-
-        @pl.when(((p == 0) | (p == last)) & (u >= nch))
-        def _():
-            low = jnp.minimum(2 * (u - nch), u - 1)
-            some(deliver_event, low, jnp.minimum(2 * (u + 1 - nch), u))
-
         @pl.when(u < begins[0])
         def _():
             per = -(-tiles // begins[0])
@@ -539,9 +500,52 @@
         @pl.when((u >= begins[0]) & (u < ends[-1]))
         def _():
             compute(u)
+
+        @pl.when((p != z) & (u < items * nch))
+        def _():
+            column_event(u)
+
+        @pl.when(u == 2)
+        def _():
+            share_stats()
+
+        @pl.when(u < 2)
+        def _():
+            some(lambda j: own_sends(j, 0), 1 + AHEAD * u, 1 + AHEAD * (u + 1))
+
+        @pl.when(u >= 2)
+        def _():
+            low = 1 + 2 * AHEAD + 3 * (u - 2)
+            some(
+                lambda j: own_sends(j, 0), jnp.minimum(low, nch), jnp.minimum(low + 3, nch)
+            )
+
+        @pl.when((u >= 3) & (u < 3 + nch))
+        def _():
+            some(gather_event, 2 * u - 6, 2 * u - 4)
+
+        corner = 4 * q + 1
+
+        @pl.when((u >= corner) & (u < corner + q))
+        def _():
+            some(corner_event, 3 * (u - corner), 3 * (u - corner) + 3)
+
+        @pl.when((p == z) & (u >= lag) & (u < lag + 2 * nch))
+        def _():
+            source_event(u - lag)
+
+        @pl.when(((p == 0) | (p == last)) & (u >= LATE) & (u < LATE + items * nch))
+        def _():
+            pass_event(u - LATE)
+
+        @pl.when(((p == 0) | (p == last)) & (u >= nch))
+        def _():
+            low = jnp.minimum(2 * (u - nch), u - LATE)
+            some(deliver_event, low, jnp.minimum(2 * (u + 1 - nch), u + 1 - LATE))
+
         return 0
 
-    lax.fori_loop(0, items * nch + 1, step, 0)
+    lax.fori_loop(0, items * nch + LATE, step, 0)
 
     @pl.when(p != z)
     def _():
@@ -744,7 +748,7 @@
     held = 4 * width * half + 2 * rows * (width + half + 256) + 12 * n * half + 4 * n * width
     return (
         row_count == 2 * feat_count and (feat_count - 1).bit_length() == 2
-        and feat_count & (feat_count - 1) == 0 and n % (3 * CHUNK) == 0 and n // CHUNK >= 3 * AHEAD + 3
+        and feat_count & (feat_count - 1) == 0 and n % (3 * CHUNK) == 0 and n // CHUNK >= 2 * AHEAD + 1
         and n <= 1024 and half % TILE == 0 and held <= VMEM_BUDGET
     )
 

time: 146 us -> 136 us (0.932)
  Pallas kernels: 143 us -> 134 us
    pallas_call x1, Pallas kernels: 130 us -> 120 us  [line_stage(): pl.pallas_call(functools.partial(line_kernel, row_count, feat_count), out...]
where the time goes in v6:
time: 136 us; the launch traced here: 134 us
  Pallas kernels  134 us (99%)
    pallas_call x1, Pallas kernels, line_stage(): pl.pallas_call(functools.partial(line_kernel, row_count, feat_count), out...  120 us
    pallas_call x1, Pallas kernels, last_stage(): pl.pallas_call(last_kernel, out_shape=(pltpu.HBM((width, half), jnp.float...  13.4 us

profile of v6, /device:TPU:24, one launch (start us, length us, event | category | flops | bytes accessed | tf_op | source)
XLA Modules:
  0.0 134.2 jit_solution(18235787702654932387)
XLA Ops:
  0.6 120.1 %line_stage.1 = (f32[4096,2048]{1,0:T(8,128)S(1)}, bf16[4096,256]{1,0:T(8,128)(2,1)}, bf16[256,2048]{1,0:T(8,128)(2,1)}, f32[8,4096]{1,0:T(8,128)}) custom-call(bf16[192,4096]{1,0:T(8,128)(2,1)} %x_ref.1, s32[1,192]{1,0:T(1,128)} %bitcast.6, bf16[32,128]{1,0:T(8,128)(2,1)} %bitcast.5, f32[1,4096]{1,0:T(1,128)} %bitcast.4), custom_call_target="tpu_custom_call" | custom-call | tf_op jit(solution)/shard_map/line_stage/pallas_call | solution.py:625
  120.7 13.4 %last_stage.1 = (f32[4096,2048]{1,0:T(8,128)}, f32[1,4096]{1,0:T(1,128)}) custom-call(f32[4096,2048]{1,0:T(8,128)S(1)} %get-tuple-element.8.h_ref, bf16[4096,256]{1,0:T(8,128)(2,1)} %get-tuple-element.9.turned_ref, bf16[256,2048]{1,0:T(8,128)(2,1)} %get-tuple-element.10.cols_ref, f32[8,4096]{1,0:T(8,128)} %get-tuple-element.11.gacc_ref), custom_call_target="tpu_custom_call" | custom-call | tf_op jit(solution)/shard_map/last_stage/pallas_call | solution.py:723

commit v7 on v6

--- a/solution.py
+++ b/solution.py
@@ -50,7 +50,7 @@
 
 def line_kernel(
     row_count, feat_count, x_ref, label_ref, post_ref, prec_ref,
-    h_ref, turned_out, cols_out, pull_out,
+    h_ref, turned_out, pull_out,
     all_ref, col_ref, wr_ref, gacc_ref, kept, even, odd, abuf, st_ref, stat_ref,
     agr, pr, br, ar, adr, own_s, relay_s, extra_s, part_s, src_s, bf_s, af_s, ad_s,
     ss, sr, ts, tr, lsem,
@@ -63,7 +63,7 @@
     half = width // 2
     m = CHUNK
     nch = n // m
-    avoid = jnp.where(z == 0, 0, jnp.where(z == last, last, -1))
+    avoid = jnp.where(z == 0, 0, jnp.where(z == last, last, -8))
     relays = p != avoid
     relays_all = (p ^ last) == avoid
     has_down, has_up = z >= 1, z <= last - 1
@@ -173,9 +173,9 @@
                 ).start()
 
     def own_sends(j, _):
+        own_line(j)
         own_plane(2 * j)
         own_plane(2 * j + 1)
-        own_line(j)
         return 0
 
     own_sends(0, 0)
@@ -350,8 +350,8 @@
     third = n // 3
     once = col_ref.at[pl.ds(0, 2 * third)]
     q = nch // 3
-    begins = [3 * q, 4 * q + 1, 5 * q + 1, 6 * q, 7 * q, 8 * q]
-    ends = [4 * q, 5 * q + 1, 6 * q, 7 * q, 8 * q, 9 * q]
+    begins = [2 * q + 1, 4 * q + 1, 5 * q + 1, 6 * q, 7 * q, 8 * q]
+    ends = [4 * q - 1, 5 * q + 1, 6 * q, 7 * q, 8 * q, 9 * q]
     near, far = pick(p, 1, edge), pick(p, 2, edge)
 
     def partner_rows(chip):
@@ -542,7 +542,6 @@
         def _():
             low = jnp.minimum(2 * (u - nch), u - LATE)
             some(deliver_event, low, jnp.minimum(2 * (u + 1 - nch), u + 1 - LATE))
-
         return 0
 
     lax.fori_loop(0, items * nch + LATE, step, 0)
@@ -552,13 +551,11 @@
         remote(once, once, bf_s.at[0], adr.at[2], rows=r).wait_recv()
 
     outs = [pltpu.make_async_copy(gacc_ref, pull_out, lsem.at[4])]
-    for i, start in enumerate(unit_rows(jnp.int32(2))):
-        outs.append(pltpu.make_async_copy(
-            col_ref.at[pl.ds(pl.multiple_of(start, CHUNK), third)],
-            cols_out.at[pl.ds(i * third, third)], lsem.at[5 + i],
-        ))
     for copy in outs:
         copy.start()
+    for i, start in enumerate(unit_rows(jnp.int32(2))):
+        held = col_ref[pl.ds(pl.multiple_of(start, CHUNK), third), :]
+        h_ref[pl.ds(width + i * third, third), :] = held.astype(jnp.float32)
 
     def sent(ref, sem):
         remote(ref, ref, sem, pr.at[3], rows=r).wait_send()
@@ -625,9 +622,8 @@
     return pl.pallas_call(
         functools.partial(line_kernel, row_count, feat_count),
         out_shape=(
-            pltpu.VMEM((width, half), jnp.float32),
+            pltpu.VMEM((width + 4 * n // 3, half), jnp.float32),
             pltpu.HBM((width, 4 * n // 3), features.dtype),
-            pltpu.HBM((4 * n // 3, half), features.dtype),
             pltpu.HBM((8, width), jnp.float32),
         ),
         in_specs=[
@@ -635,7 +631,7 @@
             pl.BlockSpec(memory_space=pltpu.VMEM), pl.BlockSpec(memory_space=pltpu.VMEM),
         ],
         out_specs=[pl.BlockSpec(memory_space=pltpu.VMEM)]
-        + [pl.BlockSpec(memory_space=pl.ANY)] * 3,
+        + [pl.BlockSpec(memory_space=pl.ANY)] * 2,
         scratch_shapes=[
             pltpu.VMEM((row_count * n, width), features.dtype),
             pltpu.VMEM((row_count * n, half), features.dtype),
@@ -656,21 +652,19 @@
             dma((9,)),
         ],
         compiler_params=pltpu.CompilerParams(
-            collective_id=0, has_side_effects=True, vmem_limit_bytes=30 * 1024 * 1024
+            collective_id=0, has_side_effects=True, vmem_limit_bytes=28 * 1024 * 1024
         ),
         name="line_stage",
     )(features, labels, post, prec)
 
 
 def last_kernel(
-    h_ref, turned_ref, cols_ref, gacc_ref,
+    h_ref, turned_ref, gacc_ref,
     out_ref, grad_ref, stage, turned, cols, gacc, grad, sem, lsem, tsem,
 ):
-    width, half = h_ref.shape
+    width, half = out_ref.shape
     slots = stage.shape[0]
     count = width // PART
-    load = pltpu.make_async_copy(cols_ref, cols, lsem.at[0])
-    load.start()
 
     def part_of(i):
         return pl.ds(pl.multiple_of(i * PART, PART), PART)
@@ -688,7 +682,7 @@
         take(i).start()
     late = pltpu.make_async_copy(gacc_ref, gacc, lsem.at[1])
     late.start()
-    load.wait()
+    cols[...] = h_ref[pl.ds(width, cols.shape[0]), :].astype(cols.dtype)
 
     def one(i, _):
         @pl.when(i >= slots)
@@ -715,11 +709,11 @@
     give.wait()
 
 
-def last_stage(h, turned, cols, gacc):
-    width, half = h.shape
+def last_stage(h, turned, gacc):
+    width, half = turned.shape[0], h.shape[1]
     dma = pltpu.SemaphoreType.DMA
     h = pltpu.with_memory_space_constraint(h, pltpu.VMEM)
-    kept = [pltpu.with_memory_space_constraint(a, pltpu.HBM) for a in (turned, cols, gacc)]
+    kept = [pltpu.with_memory_space_constraint(a, pltpu.HBM) for a in (turned, gacc)]
     return pl.pallas_call(
         last_kernel,
         out_shape=(
@@ -727,12 +721,12 @@
             pltpu.HBM((1, width), jnp.float32),
         ),
         in_specs=[pl.BlockSpec(memory_space=pltpu.VMEM)]
-        + [pl.BlockSpec(memory_space=pl.ANY)] * 3,
+        + [pl.BlockSpec(memory_space=pl.ANY)] * 2,
         out_specs=[pl.BlockSpec(memory_space=pl.ANY)] * 2,
         scratch_shapes=[
             pltpu.VMEM((3, PART, half), jnp.float32),
             pltpu.VMEM(turned.shape, turned.dtype),
-            pltpu.VMEM(cols.shape, cols.dtype),
+            pltpu.VMEM((h.shape[0] - width, half), turned.dtype),
             pltpu.VMEM(gacc.shape, gacc.dtype),
             pltpu.VMEM((1, width), jnp.float32),
             dma((3,)), dma((3,)), dma((width // PART,)),
@@ -748,7 +742,7 @@
     held = 4 * width * half + 2 * rows * (width + half + 256) + 12 * n * half + 4 * n * width
     return (
         row_count == 2 * feat_count and (feat_count - 1).bit_length() == 2
-        and feat_count & (feat_count - 1) == 0 and n % (3 * CHUNK) == 0 and n // CHUNK >= 2 * AHEAD + 1
+        and feat_count & (feat_count - 1) == 0 and n % (6 * CHUNK) == 0 and n // CHUNK >= 2 * AHEAD + 1
         and n <= 1024 and half % TILE == 0 and held <= VMEM_BUDGET
     )
 

time: 136 us -> 134 us (0.985)
  Pallas kernels: 134 us -> 131 us
where the time goes in v7:
time: 134 us; the launch traced here: 132 us
  Pallas kernels  131 us (98%)
    pallas_call x1, Pallas kernels, line_stage(): pl.pallas_call(functools.partial(line_kernel, row_count, feat_count), out...  119 us
    pallas_call x1, Pallas kernels, last_stage(): pl.pallas_call(last_kernel, out_shape=(pltpu.HBM((width, half), jnp.float...  12.4 us

profile of v7, /device:TPU:24, one launch (start us, length us, event | category | flops | bytes accessed | tf_op | source)
XLA Modules:
  0.0 132.0 jit_solution(10586779328310932144)
XLA Ops:
  0.6 118.9 %line_stage.1 = (f32[4352,2048]{1,0:T(8,128)S(1)}, bf16[4096,256]{1,0:T(8,128)(2,1)}, f32[8,4096]{1,0:T(8,128)}) custom-call(bf16[192,4096]{1,0:T(8,128)(2,1)} %x_ref.1, s32[1,192]{1,0:T(1,128)} %bitcast.6, bf16[32,128]{1,0:T(8,128)(2,1)} %bitcast.5, f32[1,4096]{1,0:T(1,128)} %bitcast.4), custom_call_target="tpu_custom_call" | custom-call | tf_op jit(solution)/shard_map/line_stage/pallas_call | solution.py:622
  119.6 12.4 %last_stage.1 = (f32[4096,2048]{1,0:T(8,128)}, f32[1,4096]{1,0:T(1,128)}) custom-call(f32[4352,2048]{1,0:T(8,128)S(1)} %get-tuple-element.7.h_ref, bf16[4096,256]{1,0:T(8,128)(2,1)} %get-tuple-element.8.turned_ref, f32[8,4096]{1,0:T(8,128)} %get-tuple-element.9.gacc_ref), custom_call_target="tpu_custom_call" | custom-call | tf_op jit(solution)/shard_map/last_stage/pallas_call | solution.py:717

commit v8 on v7

--- a/solution.py
+++ b/solution.py
@@ -10,6 +10,7 @@
 MESH = pl.DeviceIdType.MESH
 SPLIT = 2
 CHUNK = 16
+PIECES = 4
 TILE = 512
 PART = 256
 AHEAD = 2
@@ -30,7 +31,7 @@
 def slabs(ref, lead, starts, size, cols):
     parts = []
     for start in starts:
-        rows = pl.ds(pl.multiple_of(start, CHUNK), size)
+        rows = pl.ds(pl.multiple_of(start, 16), size)
         parts.append(ref[rows, cols] if lead is None else ref[lead, rows, cols])
     return jnp.concatenate(parts, axis=0)
 
@@ -53,7 +54,7 @@
     h_ref, turned_out, pull_out,
     all_ref, col_ref, wr_ref, gacc_ref, kept, even, odd, abuf, st_ref, stat_ref,
     agr, pr, br, ar, adr, own_s, relay_s, extra_s, part_s, src_s, bf_s, af_s, ad_s,
-    ss, sr, ts, tr, lsem,
+    side_r, side_s, ss, sr, ts, tr, lsem,
 ):
     r = lax.axis_index("rows")
     z = lax.axis_index("feat")
@@ -63,6 +64,9 @@
     half = width // 2
     m = CHUNK
     nch = n // m
+    items = last
+    big = n // PIECES
+    pace = nch // (3 * PIECES)
     avoid = jnp.where(z == 0, 0, jnp.where(z == last, last, -8))
     relays = p != avoid
     relays_all = (p ^ last) == avoid
@@ -73,6 +77,9 @@
 
     def own_rows(j):
         return pl.ds(pl.multiple_of(j * m, m), m)
+
+    def big_rows(chip, core, j):
+        return pl.ds(pl.multiple_of((chip * 2 + core) * n + j * big, 16), big)
 
     def cols_of(h):
         return pl.ds(pl.multiple_of(h * half, half), half)
@@ -108,7 +115,7 @@
         count = min(128, n - 128 * t)
         here = pl.ds(128 * t, count)
         st_ref[8 + t:9 + t, 0:count] = label_ref[:, here].astype(jnp.float32)
-        rows = pl.ds(pl.multiple_of(r * n + 128 * t, CHUNK), count)
+        rows = pl.ds(pl.multiple_of(r * n + 128 * t, 16), count)
 
         total = jnp.zeros((count, 128), jnp.float32)
         for i in range(width // 128):
@@ -123,22 +130,23 @@
 
     def ag(dim, h, j, src, chip, rel, send):
         remote(
-            src, all_ref.at[rows_of(chip, c, j), cols_of(h)],
+            src, all_ref.at[big_rows(chip, c, j), cols_of(h)],
             send, agr.at[rel, h, j], rows=r ^ (2 * dim),
         ).start()
 
     def own_plane(s):
-        j = lax.rem(s, nch)
-
-        @pl.when(s < nch)
-        def _():
-            ag(1, 0, j, x_ref.at[own_rows(j), cols_of(0)], p, 0, own_s.at[0])
-            ag(2, 1, j, x_ref.at[own_rows(j), cols_of(1)], p, 1, own_s.at[1])
-
-        @pl.when(s >= nch)
-        def _():
-            ag(1, 1, j, x_ref.at[own_rows(j), cols_of(1)], p, 0, own_s.at[0])
-            ag(2, 0, j, x_ref.at[own_rows(j), cols_of(0)], p, 1, own_s.at[1])
+        j = lax.rem(s, PIECES)
+        rows = pl.ds(pl.multiple_of(j * big, 16), big)
+
+        @pl.when(s < PIECES)
+        def _():
+            ag(1, 0, j, x_ref.at[rows, cols_of(0)], p, 0, own_s.at[0])
+            ag(2, 1, j, x_ref.at[rows, cols_of(1)], p, 1, own_s.at[1])
+
+        @pl.when(s >= PIECES)
+        def _():
+            ag(1, 1, j, x_ref.at[rows, cols_of(1)], p, 0, own_s.at[0])
+            ag(2, 0, j, x_ref.at[rows, cols_of(0)], p, 1, own_s.at[1])
 
     def own_line(j):
         for h in range(2):
@@ -174,8 +182,11 @@
 
     def own_sends(j, _):
         own_line(j)
-        own_plane(2 * j)
-        own_plane(2 * j + 1)
+
+        @pl.when(lax.rem(j, 3 * pace) == 0)
+        def _():
+            own_plane(2 * (j // (3 * pace)))
+            own_plane(2 * (j // (3 * pace)) + 1)
         return 0
 
     own_sends(0, 0)
@@ -223,7 +234,7 @@
                 turned = value.astype(jnp.float32).T
                 for t in range(-(-n // 128)):
                     count = min(128, n - 128 * t)
-                    rows = pl.ds(pl.multiple_of(i * n + 128 * t, CHUNK), count)
+                    rows = pl.ds(pl.multiple_of(i * n + 128 * t, 16), count)
                     wr_ref[lead, rows, :] = jnp.broadcast_to(
                         turned[:count, t:t + 1], (count, 128)
                     ).astype(jnp.bfloat16)
@@ -233,17 +244,17 @@
 
     def arrive(rel, h, j):
         chip = p ^ (rel + 1)
-        here = all_ref.at[rows_of(chip, c, j), cols_of(h)]
+        here = all_ref.at[big_rows(chip, c, j), cols_of(h)]
         remote(here, here, own_s.at[0], agr.at[rel, h, j], rows=r).wait_recv()
         remote(here, here, part_s.at[rel], pr.at[rel], rows=r ^ 1).start()
 
     def forward(rel, h, j, send):
         chip = p ^ (rel + 1)
-        here = all_ref.at[rows_of(chip, c, j), cols_of(h)]
+        here = all_ref.at[big_rows(chip, c, j), cols_of(h)]
         ag(2 - rel, h, j, here, chip, 2, send)
 
     def gather_event(s):
-        a, j = s // nch, s % nch
+        a, j = s // PIECES, s % PIECES
 
         @pl.when(a == 0)
         def _():
@@ -302,11 +313,44 @@
             here = col_ref.at[rows_of(chip, k, j)]
             remote(here, here, bf_s.at[q], br.at[q, k, j], rows=r).wait_recv()
 
-            @pl.when((down & has_down) | (~down & has_up))
+            rest = (s < items * nch - 1) | ((p != 0) & (p != last))
+
+            @pl.when(((down & has_down) | (~down & has_up)) & rest)
             def _():
                 remote(
                     here, here, bf_s.at[q], br.at[q, k, j],
                     feat=jnp.where(down, z - 1, z + 1),
+                ).start()
+
+    side_down, side_up = (p ^ 2) == last, p == 2
+    side_first = (side_down & (z == last)) | (side_up & (z == 0))
+    side_later = (side_down & (z < last)) | (side_up & (z > 0))
+    side_more = (side_down & has_down) | (side_up & has_up)
+    side_give = (side_down & (z <= last - 2)) | (side_up & (z >= 2))
+    side_next = jnp.where(side_down, z - 1, z + 1)
+    side_rows = own_rows(nch - 1)
+
+    def side_own():
+        for h in range(2):
+            remote(
+                x_ref.at[side_rows, cols_of(h)], abuf.at[0, c, side_rows],
+                side_s.at[0], side_r.at[c], rows=2 * p + h, feat=side_next,
+            ).start()
+
+    def side_event():
+        for k in range(2):
+            here = abuf.at[0, k, side_rows]
+            remote(here, here, side_s.at[1], side_r.at[k], rows=r).wait_recv()
+
+            @pl.when(side_more)
+            def _():
+                remote(here, here, side_s.at[1], side_r.at[k], feat=side_next).start()
+
+            @pl.when(side_give)
+            def _():
+                remote(
+                    here, col_ref.at[rows_of(p, k, nch - 1)], side_s.at[2],
+                    br.at[items - 1, k, nch - 1], rows=2 * (p ^ 2) + c,
                 ).start()
 
     def pass_event(s):
@@ -342,8 +386,7 @@
                     ad_s.at[q], adr.at[j // (nch // 3)], rows=2 * block + c,
                 ).start()
 
-    items = last
-    lag = nch // 2 + 3
+    lag = 10 * pace
     tiles = width // TILE
     edge = passed_chip(p, z, last)
     twice = col_ref.at[pl.ds(0, 2 * n)]
@@ -351,7 +394,7 @@
     once = col_ref.at[pl.ds(0, 2 * third)]
     q = nch // 3
     begins = [2 * q + 1, 4 * q + 1, 5 * q + 1, 6 * q, 7 * q, 8 * q]
-    ends = [4 * q - 1, 5 * q + 1, 6 * q, 7 * q, 8 * q, 9 * q]
+    ends = [4 * q - 1, 5 * q + 1, 6 * q, 7 * q, 8 * q, 9 * q - pace]
     near, far = pick(p, 1, edge), pick(p, 2, edge)
 
     def partner_rows(chip):
@@ -485,6 +528,10 @@
         def _():
             lax.fori_loop(low, high, pair, 0)
 
+        @pl.when(u == ends[-1] - 1)
+        def _():
+            pltpu.make_async_copy(gacc_ref, pull_out, lsem.at[4]).start()
+
     def some(event, low, high):
         def one(i, _):
             event(i)
@@ -520,15 +567,26 @@
                 lambda j: own_sends(j, 0), jnp.minimum(low, nch), jnp.minimum(low + 3, nch)
             )
 
-        @pl.when((u >= 3) & (u < 3 + nch))
-        def _():
-            some(gather_event, 2 * u - 6, 2 * u - 4)
-
-        corner = 4 * q + 1
-
-        @pl.when((u >= corner) & (u < corner + q))
-        def _():
-            some(corner_event, 3 * (u - corner), 3 * (u - corner) + 3)
+        @pl.when((u == 0) & side_first)
+        def _():
+            side_own()
+        hops = jnp.where(side_down, last - z, z)
+
+        @pl.when((u == 3 * hops + 4) & side_later)
+        def _():
+            side_event()
+        for e in range(2):
+            i = u - (4 + 2 * e) * pace
+
+            @pl.when((i >= 0) & (i % (3 * pace) == 0) & (i < 3 * pace * PIECES))
+            def _():
+                gather_event(2 * (i // (3 * pace)) + e)
+
+        corner = u - 4 * q - 1
+
+        @pl.when((corner >= 0) & (corner < q) & (corner % pace == 0))
+        def _():
+            corner_event(corner // pace)
 
         @pl.when((p == z) & (u >= lag) & (u < lag + 2 * nch))
         def _():
@@ -550,11 +608,8 @@
     def _():
         remote(once, once, bf_s.at[0], adr.at[2], rows=r).wait_recv()
 
-    outs = [pltpu.make_async_copy(gacc_ref, pull_out, lsem.at[4])]
-    for copy in outs:
-        copy.start()
     for i, start in enumerate(unit_rows(jnp.int32(2))):
-        held = col_ref[pl.ds(pl.multiple_of(start, CHUNK), third), :]
+        held = col_ref[pl.ds(pl.multiple_of(start, 16), third), :]
         h_ref[pl.ds(width + i * third, third), :] = held.astype(jnp.float32)
 
     def sent(ref, sem):
@@ -584,6 +639,17 @@
         sent(x_ref, own_s.at[3])
     for rel in range(4):
         sent(x_ref, part_s.at[rel])
+    @pl.when(side_first)
+    def _():
+        sent(x_ref.at[pl.ds(0, m)], side_s.at[0])
+
+    @pl.when(side_later & side_more)
+    def _():
+        sent(col_ref.at[pl.ds(0, 2 * m)], side_s.at[1])
+
+    @pl.when(side_later & side_give)
+    def _():
+        sent(col_ref.at[pl.ds(0, 2 * m)], side_s.at[2])
     down = p > z
     for q in range(items):
         if q > 0:
@@ -595,9 +661,16 @@
             def _():
                 sent(x_ref, src_s.at[1, q])
 
-        @pl.when((p != z) & ((down & has_down) | (~down & has_up)))
+        sends = (p != z) & ((down & has_down) | (~down & has_up))
+        short = ((p == 0) | (p == last)) if q == items - 1 else p < 0
+
+        @pl.when(sends & ~short)
         def _():
             sent(twice, bf_s.at[q])
+
+        @pl.when(sends & short)
+        def _():
+            sent(col_ref.at[pl.ds(0, 2 * n - 2 * m)], bf_s.at[q])
         for edge, block, more in ((0, z + 1 + q, has_down), (last, z - 1 - q, has_up)):
             @pl.when((p == edge) & (block >= 0) & (block <= last))
             def _():
@@ -606,8 +679,7 @@
                 @pl.when(more)
                 def _():
                     sent(twice, af_s.at[q])
-    for copy in outs:
-        copy.wait()
+    pltpu.make_async_copy(gacc_ref, pull_out, lsem.at[4]).wait()
     pltpu.make_async_copy(kept, turned_out, lsem.at[3]).wait()
 
 
@@ -643,10 +715,10 @@
             pltpu.VMEM((items, 2, n, half), features.dtype),
             pltpu.VMEM((16, 128), jnp.float32),
             pltpu.VMEM((row_count, feat_count, 16, 128), jnp.float32),
-            dma((3, 2, nch)), dma((4,)), dma((items, 2, nch)), dma((items + 1, 2, nch)),
+            dma((3, 2, PIECES)), dma((4,)), dma((items, 2, nch)), dma((items + 1, 2, nch)),
             dma((3,)),
             dma((4,)), dma((2,)), dma((2,)), dma((4,)), dma((2, items)), dma((items,)),
-            dma((items,)), dma((items,)),
+            dma((items,)), dma((items,)), dma((2,)), dma((3,)),
             dma((feat_count,)), dma((feat_count,)),
             dma((row_count,)), dma((row_count,)),
             dma((9,)),
@@ -742,7 +814,7 @@
     held = 4 * width * half + 2 * rows * (width + half + 256) + 12 * n * half + 4 * n * width
     return (
         row_count == 2 * feat_count and (feat_count - 1).bit_length() == 2
-        and feat_count & (feat_count - 1) == 0 and n % (6 * CHUNK) == 0 and n // CHUNK >= 2 * AHEAD + 1
+        and feat_count & (feat_count - 1) == 0 and n % (3 * PIECES * CHUNK) == 0 and n // CHUNK >= 2 * AHEAD + 1
         and n <= 1024 and half % TILE == 0 and held <= VMEM_BUDGET
     )
 

time: 134 us -> 132 us (0.985)
  Pallas kernels: 131 us -> 129 us
    pallas_call x1, Pallas kernels: 119 us -> 117 us  [line_stage(): pl.pallas_call(functools.partial(line_kernel, row_count, feat_count), out...]
where the time goes in v8:
time: 132 us; the launch traced here: 130 us
  Pallas kernels  129 us (98%)
    pallas_call x1, Pallas kernels, line_stage(): pl.pallas_call(functools.partial(line_kernel, row_count, feat_count), out...  117 us
    pallas_call x1, Pallas kernels, last_stage(): pl.pallas_call(last_kernel, out_shape=(pltpu.HBM((width, half), jnp.float...  12.4 us

profile of v8, /device:TPU:24, one launch (start us, length us, event | category | flops | bytes accessed | tf_op | source)
XLA Modules:
  0.0 129.6 jit_solution(2449993256863696024)
XLA Ops:
  0.6 116.5 %line_stage.1 = (f32[4352,2048]{1,0:T(8,128)S(1)}, bf16[4096,256]{1,0:T(8,128)(2,1)}, f32[8,4096]{1,0:T(8,128)}) custom-call(bf16[192,4096]{1,0:T(8,128)(2,1)} %x_ref.1, s32[1,192]{1,0:T(1,128)} %bitcast.6, bf16[32,128]{1,0:T(8,128)(2,1)} %bitcast.5, f32[1,4096]{1,0:T(1,128)} %bitcast.4), custom_call_target="tpu_custom_call" | custom-call | tf_op jit(solution)/shard_map/line_stage/pallas_call | solution.py:694
  117.2 12.4 %last_stage.1 = (f32[4096,2048]{1,0:T(8,128)}, f32[1,4096]{1,0:T(1,128)}) custom-call(f32[4352,2048]{1,0:T(8,128)S(1)} %get-tuple-element.7.h_ref, bf16[4096,256]{1,0:T(8,128)(2,1)} %get-tuple-element.8.turned_ref, f32[8,4096]{1,0:T(8,128)} %get-tuple-element.9.gacc_ref), custom_call_target="tpu_custom_call" | custom-call | tf_op jit(solution)/shard_map/last_stage/pallas_call | solution.py:789

commit v9 on v8

--- a/solution.py
+++ b/solution.py
@@ -473,6 +473,7 @@
             return out
 
         begin, span = choose(begins), choose([e - s for s, e in zip(begins, ends)])
+        span = jnp.where((index >= 3) & (p != z) & ((z == 0) | (z == last)), span - pace, span)
         low = jnp.minimum((u - begin) * tiles // span, tiles)
         high = jnp.minimum((u - begin + 1) * tiles // span, tiles)
         rows = unit_rows(index)
@@ -523,6 +524,12 @@
             @pl.when(u == ends[2] - 1)
             def _():
                 pltpu.make_async_copy(kept, turned_out, lsem.at[3]).start()
+                depth = 4 * third
+                cut = PART * depth // half
+                for i in range(half // depth):
+                    h_ref[pl.ds(width + depth, cut), pl.ds(i * depth, depth)] = kept[
+                        pl.ds(i * cut, cut), :
+                    ].astype(jnp.float32)
 
         @pl.when(index != 2)
         def _():
@@ -681,6 +688,11 @@
                     sent(twice, af_s.at[q])
     pltpu.make_async_copy(gacc_ref, pull_out, lsem.at[4]).wait()
     pltpu.make_async_copy(kept, turned_out, lsem.at[3]).wait()
+
+
+def extra_rows(n, half):
+    depth = 4 * n // 3
+    return depth + PART * depth // half
 
 
 def line_stage(features, labels, post, prec):
@@ -694,7 +706,7 @@
     return pl.pallas_call(
         functools.partial(line_kernel, row_count, feat_count),
         out_shape=(
-            pltpu.VMEM((width + 4 * n // 3, half), jnp.float32),
+            pltpu.VMEM((width + extra_rows(n, half), half), jnp.float32),
             pltpu.HBM((width, 4 * n // 3), features.dtype),
             pltpu.HBM((8, width), jnp.float32),
         ),
@@ -750,17 +762,25 @@
         slot = lax.rem(i, slots)
         return pltpu.make_async_copy(stage.at[slot], out_ref.at[part_of(i)], sem.at[slot])
 
-    for i in range(count):
+    for i in range(1, count):
         take(i).start()
     late = pltpu.make_async_copy(gacc_ref, gacc, lsem.at[1])
     late.start()
-    cols[...] = h_ref[pl.ds(width, cols.shape[0]), :].astype(cols.dtype)
+    depth = cols.shape[0]
+    cut = PART * depth // half
+    cols[...] = h_ref[pl.ds(width, depth), :].astype(cols.dtype)
+    for i in range(half // depth):
+        turned[pl.ds(i * cut, cut), :] = h_ref[
+            pl.ds(width + depth, cut), pl.ds(i * depth, depth)
+        ].astype(turned.dtype)
 
     def one(i, _):
         @pl.when(i >= slots)
         def _():
             put(i - slots).wait()
-        take(i).wait()
+        @pl.when(i >= 1)
+        def _():
+            take(i).wait()
         slot = lax.rem(i, slots)
         value = turned[part_of(i), :]
         for t in range(half // TILE):
@@ -798,7 +818,7 @@
         scratch_shapes=[
             pltpu.VMEM((3, PART, half), jnp.float32),
             pltpu.VMEM(turned.shape, turned.dtype),
-            pltpu.VMEM((h.shape[0] - width, half), turned.dtype),
+            pltpu.VMEM((turned.shape[1], half), turned.dtype),
             pltpu.VMEM(gacc.shape, gacc.dtype),
             pltpu.VMEM((1, width), jnp.float32),
             dma((3,)), dma((3,)), dma((width // PART,)),
@@ -815,6 +835,7 @@
     return (
         row_count == 2 * feat_count and (feat_count - 1).bit_length() == 2
         and feat_count & (feat_count - 1) == 0 and n % (3 * PIECES * CHUNK) == 0 and n // CHUNK >= 2 * AHEAD + 1
+        and half % (4 * n // 3) == 0 and PART * (4 * n // 3) % (16 * half) == 0
         and n <= 1024 and half % TILE == 0 and held <= VMEM_BUDGET
     )
 

time: 132 us -> 130 us (0.985)
  no operation moved by 1% of the time
where the time goes in v9:
time: 130 us; the launch traced here: 129 us
  Pallas kernels  128 us (98%)
    pallas_call x1, Pallas kernels, line_stage(): pl.pallas_call(functools.partial(line_kernel, row_count, feat_count), out...  116 us
    pallas_call x1, Pallas kernels, last_stage(): pl.pallas_call(last_kernel, out_shape=(pltpu.HBM((width, half), jnp.float...  11.7 us

profile of v9, /device:TPU:24, one launch (start us, length us, event | category | flops | bytes accessed | tf_op | source)
XLA Modules:
  0.0 128.8 jit_solution(6497759245760458758)
XLA Ops:
  0.6 116.4 %line_stage.1 = (f32[4384,2048]{1,0:T(8,128)S(1)}, bf16[4096,256]{1,0:T(8,128)(2,1)}, f32[8,4096]{1,0:T(8,128)}) custom-call(bf16[192,4096]{1,0:T(8,128)(2,1)} %x_ref.1, s32[1,192]{1,0:T(1,128)} %bitcast.6, bf16[32,128]{1,0:T(8,128)(2,1)} %bitcast.5, f32[1,4096]{1,0:T(1,128)} %bitcast.4), custom_call_target="tpu_custom_call" | custom-call | tf_op jit(solution)/shard_map/line_stage/pallas_call | solution.py:706
  117.0 11.7 %last_stage.1 = (f32[4096,2048]{1,0:T(8,128)}, f32[1,4096]{1,0:T(1,128)}) custom-call(f32[4384,2048]{1,0:T(8,128)S(1)} %get-tuple-element.7.h_ref, bf16[4096,256]{1,0:T(8,128)(2,1)} %get-tuple-element.8.turned_ref, f32[8,4096]{1,0:T(8,128)} %get-tuple-element.9.gacc_ref), custom_call_target="tpu_custom_call" | custom-call | tf_op jit(solution)/shard_map/last_stage/pallas_call | solution.py:809
